TPU v7x, 1024 devices: a whole 8x8x8 slice. The times are simulated.
1024 devices in a mesh: seq: 16 (over y, core), dp: 64 (over x, z).
Axes of the slice: x: 8, y: 8, z: 8, core: 2. Of those that a mesh axis runs over, the one named last changes fastest.
Arguments:
- queries: bfloat16 [64, 2048, 512], P('dp', 'seq'), may hold values from -6 to 6
- keys: bfloat16 [64, 2048, 512], P('dp', 'seq'), may hold values from -6 to 6
- values: bfloat16 [64, 2048, 512], P('dp', 'seq'), may hold values from -6 to 6
- alpha: float32 [64, 2048, 4], P('dp', 'seq'), may hold values from -4 to 100000
- beta: float32 [64, 2048, 4], P('dp', 'seq'), may hold values from 0.05 to 0.2
- log_rate: float32 [4], replicated, may hold values from -12 to -3
- grad_out: bfloat16 [64, 2048, 512], P('dp', 'seq'), may hold values from -6 to 6
Outputs:
- outputs: bfloat16 [64, 2048, 512], P('dp', 'seq')
- grad_queries: bfloat16 [64, 2048, 512], P('dp', 'seq')
- grad_keys: bfloat16 [64, 2048, 512], P('dp', 'seq')
- grad_values: bfloat16 [64, 2048, 512], P('dp', 'seq')
- grad_alpha: float32 [64, 2048, 4], P('dp', 'seq')
- grad_beta: float32 [64, 2048, 4], P('dp', 'seq')
- grad_log_rate: float32 [4], replicated
All inputs are finite; a program needn't handle non-finite values.
Results may differ from a plain program's by a relative error of at most 0.001.
Values sent between devices are 32-bit elements; how exact they have to be, the bound alone decides.
A program may use at most 64 MiB of HBM per device.

v0:
```python
import functools

import jax
import jax.numpy as jnp
from jax import lax
from jax.sharding import Mesh
from jax.sharding import PartitionSpec as P

H = 4
DK = 128
DV = 128
BLOCK = 64
SEQ = ("seq_0", "seq_1")
SEQ_DP = ("seq_0", "seq_1", "dp_0", "dp_1")
DP = ("dp_0", "dp_1")


EPSILON = 1e-06
highest = lax.Precision.HIGHEST


def passed_along(value, axis, steps):
    count = lax.axis_size(axis)
    first, last = (max(0, -steps), min(count, count - steps))
    return lax.ppermute(value, axis, [(source, source + steps) for source in range(first, last)])


def by_axis(x, axes):
    return functools.reduce(lax.psum, axes, x)


def to_blocks(tensor, blocks_count):
    moved = tensor.reshape((blocks_count, BLOCK) + tensor.shape[1:])
    return jnp.moveaxis(moved, 2, 0)


def recurrence(queries_n, keys_n, values_n, log_gate, betas, initial, with_output):
    length = keys_n.shape[0]
    blocks_count = length // BLOCK
    query_b = to_blocks(queries_n, blocks_count)
    key_b = to_blocks(keys_n, blocks_count)
    value_b = to_blocks(values_n, blocks_count)
    gate_b = to_blocks(log_gate, blocks_count)
    beta_b = to_blocks(betas, blocks_count)
    cumulated = jnp.cumsum(gate_b, axis=-1)
    spread = cumulated[..., :, None] - cumulated[..., None, :]
    row_ids = lax.broadcasted_iota(jnp.int32, (BLOCK, BLOCK), 0)
    col_ids = lax.broadcasted_iota(jnp.int32, (BLOCK, BLOCK), 1)
    inside = jnp.exp(jnp.where(row_ids >= col_ids, spread, -jnp.inf))
    strictly = jnp.where(row_ids > col_ids, inside, 0.0)
    key_gram = jnp.einsum("hncd,hnsd->hncs", key_b, key_b, precision=highest)
    system = jnp.eye(BLOCK, dtype=key_b.dtype) + beta_b[..., None] * strictly * key_gram
    decayed = jnp.exp(cumulated)
    value_part = jax.scipy.linalg.solve_triangular(
        system, beta_b[..., None] * value_b, lower=True, unit_diagonal=True
    )
    key_part = jax.scipy.linalg.solve_triangular(
        system, (beta_b * decayed)[..., None] * key_b, lower=True, unit_diagonal=True
    )
    to_end = jnp.exp(cumulated[..., -1:] - cumulated)
    key_end = key_b * to_end[..., None]
    block_decay = decayed[..., -1]
    sequence = [value_part, key_part, key_end, block_decay]
    if with_output:
        query_scores = jnp.einsum("hncd,hnsd->hncs", query_b, key_b, precision=highest) * inside
        sequence = sequence + [query_b * decayed[..., None], query_scores]
    moved_in = [jnp.moveaxis(member, 1, 0) for member in sequence]

    def advance(carried, inputs):
        correction = inputs[0] - jnp.einsum("hcd,hde->hce", inputs[1], carried, precision=highest)
        updated = inputs[3][:, None, None] * carried + jnp.einsum(
            "hcd,hce->hde", inputs[2], correction, precision=highest
        )
        if with_output:
            emitted = jnp.einsum("hcd,hde->hce", inputs[4], carried, precision=highest)
            emitted = emitted + jnp.einsum("hcs,hse->hce", inputs[5], correction, precision=highest)
            return (updated, emitted)
        return (updated, jnp.zeros((), carried.dtype))

    final_state, emitted = lax.scan(advance, initial, moved_in)
    if not with_output:
        return (None, final_state)
    head_count = emitted.shape[1]
    value_width = emitted.shape[3]
    result = jnp.transpose(emitted, (0, 2, 1, 3)).reshape(length, head_count * value_width)
    return (result, final_state)


def prepared(query_f, key_f, alpha_f, log_rate):
    length = query_f.shape[0]

    def normalize(tensor):
        shaped = tensor.reshape(length, H, DK)
        return shaped * lax.rsqrt(jnp.sum(shaped * shaped, axis=-1, keepdims=True) + EPSILON)

    log_gate = -jnp.exp(log_rate)[None, :] * jax.nn.softplus(alpha_f)
    return (normalize(query_f), normalize(key_f), log_gate)


def layer(query_f, key_f, value_f, alpha_f, beta_f, log_rate, initial):
    length = query_f.shape[0]
    queries_n, keys_n, log_gate = prepared(query_f, key_f, alpha_f, log_rate)
    return recurrence(
        queries_n, keys_n, value_f.reshape(length, H, DV), log_gate, beta_f, initial, True
    )


def local(queries, keys, values, alpha, beta, log_rate, grad_out):
    query_f = queries[0].astype(jnp.float32)
    key_f = keys[0].astype(jnp.float32)
    value_f = values[0].astype(jnp.float32)
    alpha_f = alpha[0]
    beta_f = beta[0]
    cotangent = grad_out[0].astype(jnp.float32)
    length = query_f.shape[0]
    queries_n, keys_n, log_gate = prepared(query_f, key_f, alpha_f, log_rate)
    identity_map = jnp.broadcast_to(jnp.eye(DK, dtype=jnp.float32), (H, DK, DK))
    empty_state = jnp.zeros((H, DK, DV), jnp.float32)
    widened_values = jnp.concatenate(
        [jnp.zeros((length, H, DK), jnp.float32), value_f.reshape(length, H, DV)], axis=-1
    )
    widened_start = jnp.concatenate([identity_map, empty_state], axis=-1)
    _, summary = recurrence(
        queries_n, keys_n, widened_values, log_gate, beta_f, widened_start, False
    )
    transfer = summary[..., :DK]
    offset = summary[..., DK:]

    def from_start(start_state):
        return layer(query_f, key_f, value_f, alpha_f, beta_f, log_rate, start_state)[0]

    _, start_pullback = jax.vjp(from_start, empty_state)
    (start_adjoint,) = start_pullback(cotangent)
    adjoint_map = jnp.swapaxes(transfer, 1, 2)

    def paired_turn(counter, carried):
        leaving = jnp.einsum("hij,hjk->hik", transfer, carried[0], precision=highest) + offset
        returning = (
            jnp.einsum("hij,hjk->hik", adjoint_map, carried[1], precision=highest) + start_adjoint
        )
        forward_state = passed_along(leaving, SEQ, 1)
        backward_state = passed_along(returning, SEQ, -1)
        return (forward_state, backward_state)

    incoming, outgoing = lax.fori_loop(
        0, lax.axis_size(SEQ) - 1, paired_turn, (empty_state, empty_state)
    )

    def complete(query_in, key_in, value_in, alpha_in, beta_in, rate_in):
        return layer(query_in, key_in, value_in, alpha_in, beta_in, rate_in, incoming)

    (result, _), pullback = jax.vjp(complete, query_f, key_f, value_f, alpha_f, beta_f, log_rate)
    gradients = pullback((cotangent, outgoing))
    rate_total = by_axis(gradients[5], SEQ_DP)
    return (
        result.astype(jnp.bfloat16)[None],
        gradients[0].astype(jnp.bfloat16)[None],
        gradients[1].astype(jnp.bfloat16)[None],
        gradients[2].astype(jnp.bfloat16)[None],
        gradients[3][None],
        gradients[4][None],
        rate_total,
    )


def solution(mesh):
    split = Mesh(mesh.devices.reshape(8, 2, 8, 8), ("seq_0", "seq_1", "dp_0", "dp_1"))
    in_specs = (
        P(DP, SEQ, None),
        P(DP, SEQ, None),
        P(DP, SEQ, None),
        P(DP, SEQ, None),
        P(DP, SEQ, None),
        P(),
        P(DP, SEQ, None),
    )
    out_specs = (
        P(DP, SEQ, None),
        P(DP, SEQ, None),
        P(DP, SEQ, None),
        P(DP, SEQ, None),
        P(DP, SEQ, None),
        P(DP, SEQ, None),
        P(),
    )
    return jax.shard_map(local, mesh=split, in_specs=in_specs, out_specs=out_specs, check_vma=False)
```

profile of v0, /device:TPU:16, one launch (start us, length us, event | category | flops | bytes accessed | tf_op | source)
XLA Modules:
  0.0 390.6 jit_solution(10701482630076908818)
XLA Ops:
  9.2 39.3 %custom-call.12 = f32[4,2,1,64,64]{3,4,2,1,0:T(8,128)S(1)} custom-call(f32[4,2,1,64,64]{4,3,2,1,0:T(8,128)S(1)} %add_bitcast_fusion), custom_call_target="InvertDiagBlocksLowerTriangular" | custom-call | tf_op jit(solution)/shard_map/jit(_solve_triangular)/vmap(vmap())/triangular_solve | solution.py:54
  50.8 2.4 while.91
  59.7 3.8 while.96
  64.4 196.3 %while.93 = (s32[]{:T(128)}, f32[4,128,128]{2,1,0:T(8,128)S(1)}, f32[4,128,128]{2,1,0:T(8,128)S(1)}, f32[4,128,128]{2,1,0:T(8,128)S(1)}, f32[4,128,128]{2,1,0:T(...) while((s32[]{:T(128)}, f32[4,128,128]{2,1,0:T(8,128)S(1)}, ...), condition=%wide.region_10.12_spmd, body=%wide.region_9.11_spmd.sunk | while | flops 201457664 | bytes 4194469 | solution.py:145
  65.5 1.9 collective-permute-start
  68.5 3.6 collective-permute-start.1
  73.4 3.0 collective-permute-done.1
  77.4 3.8 collective-permute-start
  82.3 7.9 %collective-permute-start.1 = (f32[4,128,128]{2,1,0:T(8,128)}, f32[4,128,128]{2,1,0:T(8,128)S(1)}, u32[]{:S(2)}, u32[]{:S(2)}) collective-permute-start(f32[4,128,128]{2,1,0:T(8,128)} %convolution_add_fusion.24), channel_id=1, source_target_pairs={{64,0},{128,64},{192,128},{256,192},{320,256},{384,320},{448,384},... | collective-permute-start | bytes 786440 | tf_op jit(solution)/shard_map/while/body/eval_jaxpr/ppermute | solution.py:25
  91.5 3.0 collective-permute-done.1
  95.6 1.9 collective-permute-start
  98.6 3.7 collective-permute-start.1
  103.5 3.0 collective-permute-done.1
  107.6 1.9 collective-permute-start
  110.6 3.7 collective-permute-start.1
  115.5 3.0 collective-permute-done.1
  119.6 1.9 collective-permute-start
  122.6 3.7 collective-permute-start.1
  127.6 3.0 collective-permute-done.1
  131.6 2.6 collective-permute-start
  135.4 3.0 collective-permute-start.1
  139.6 3.0 collective-permute-done.1
  143.7 3.8 collective-permute-start
  148.6 1.9 collective-permute-start.1
  151.6 3.1 collective-permute-done.1
  155.8 4.9 %collective-permute-start = (f32[4,128,128]{2,1,0:T(8,128)}, f32[4,128,128]{2,1,0:T(8,128)S(1)}, u32[]{:S(2)}, u32[]{:S(2)}) collective-permute-start(f32[4,128,128]{2,1,0:T(8,128)} %convolution_add_fusion.23), channel_id=1, source_target_pairs={{0,64},{64,128},{128,192},{192,256},{256,320},{320,384},{384,448},... | collective-permute-start | bytes 786440 | tf_op jit(solution)/shard_map/while/body/eval_jaxpr/ppermute | solution.py:25
  161.9 1.9 collective-permute-start.1
  163.8 4.2 %collective-permute-done.1 = f32[4,128,128]{2,1,0:T(8,128)S(1)} collective-permute-done((f32[4,128,128]{2,1,0:T(8,128)}, f32[4,128,128]{2,1,0:T(8,128)S(1)}, u32[]{:S(2)}, u32[]{:S(2)}) %collective-permute-start.1) | collective-permute-done | bytes 262176 | tf_op jit(solution)/shard_map/while/body/eval_jaxpr/ppermute | solution.py:25
  169.1 4.9 %collective-permute-start = (f32[4,128,128]{2,1,0:T(8,128)}, f32[4,128,128]{2,1,0:T(8,128)S(1)}, u32[]{:S(2)}, u32[]{:S(2)}) collective-permute-start(f32[4,128,128]{2,1,0:T(8,128)} %convolution_add_fusion.23), channel_id=1, source_target_pairs={{0,64},{64,128},{128,192},{192,256},{256,320},{320,384},{384,448},... | collective-permute-start | bytes 786440 | tf_op jit(solution)/shard_map/while/body/eval_jaxpr/ppermute | solution.py:25
  177.0 4.2 %collective-permute-done.1 = f32[4,128,128]{2,1,0:T(8,128)S(1)} collective-permute-done((f32[4,128,128]{2,1,0:T(8,128)}, f32[4,128,128]{2,1,0:T(8,128)S(1)}, u32[]{:S(2)}, u32[]{:S(2)}) %collective-permute-start.1) | collective-permute-done | bytes 262176 | tf_op jit(solution)/shard_map/while/body/eval_jaxpr/ppermute | solution.py:25
  182.3 4.9 %collective-permute-start = (f32[4,128,128]{2,1,0:T(8,128)}, f32[4,128,128]{2,1,0:T(8,128)S(1)}, u32[]{:S(2)}, u32[]{:S(2)}) collective-permute-start(f32[4,128,128]{2,1,0:T(8,128)} %convolution_add_fusion.23), channel_id=1, source_target_pairs={{0,64},{64,128},{128,192},{192,256},{256,320},{320,384},{384,448},... | collective-permute-start | bytes 786440 | tf_op jit(solution)/shard_map/while/body/eval_jaxpr/ppermute | solution.py:25
  190.3 4.2 %collective-permute-done.1 = f32[4,128,128]{2,1,0:T(8,128)S(1)} collective-permute-done((f32[4,128,128]{2,1,0:T(8,128)}, f32[4,128,128]{2,1,0:T(8,128)S(1)}, u32[]{:S(2)}, u32[]{:S(2)}) %collective-permute-start.1) | collective-permute-done | bytes 262176 | tf_op jit(solution)/shard_map/while/body/eval_jaxpr/ppermute | solution.py:25
  195.6 4.9 %collective-permute-start = (f32[4,128,128]{2,1,0:T(8,128)}, f32[4,128,128]{2,1,0:T(8,128)S(1)}, u32[]{:S(2)}, u32[]{:S(2)}) collective-permute-start(f32[4,128,128]{2,1,0:T(8,128)} %convolution_add_fusion.23), channel_id=1, source_target_pairs={{0,64},{64,128},{128,192},{192,256},{256,320},{320,384},{384,448},... | collective-permute-start | bytes 786440 | tf_op jit(solution)/shard_map/while/body/eval_jaxpr/ppermute | solution.py:25
  203.5 4.2 %collective-permute-done.1 = f32[4,128,128]{2,1,0:T(8,128)S(1)} collective-permute-done((f32[4,128,128]{2,1,0:T(8,128)}, f32[4,128,128]{2,1,0:T(8,128)S(1)}, u32[]{:S(2)}, u32[]{:S(2)}) %collective-permute-start.1) | collective-permute-done | bytes 262176 | tf_op jit(solution)/shard_map/while/body/eval_jaxpr/ppermute | solution.py:25
  208.8 4.9 %collective-permute-start = (f32[4,128,128]{2,1,0:T(8,128)}, f32[4,128,128]{2,1,0:T(8,128)S(1)}, u32[]{:S(2)}, u32[]{:S(2)}) collective-permute-start(f32[4,128,128]{2,1,0:T(8,128)} %convolution_add_fusion.23), channel_id=1, source_target_pairs={{0,64},{64,128},{128,192},{192,256},{256,320},{320,384},{384,448},... | collective-permute-start | bytes 786440 | tf_op jit(solution)/shard_map/while/body/eval_jaxpr/ppermute | solution.py:25
  216.8 4.2 %collective-permute-done.1 = f32[4,128,128]{2,1,0:T(8,128)S(1)} collective-permute-done((f32[4,128,128]{2,1,0:T(8,128)}, f32[4,128,128]{2,1,0:T(8,128)S(1)}, u32[]{:S(2)}, u32[]{:S(2)}) %collective-permute-start.1) | collective-permute-done | bytes 262176 | tf_op jit(solution)/shard_map/while/body/eval_jaxpr/ppermute | solution.py:25
  222.0 4.9 %collective-permute-start = (f32[4,128,128]{2,1,0:T(8,128)}, f32[4,128,128]{2,1,0:T(8,128)S(1)}, u32[]{:S(2)}, u32[]{:S(2)}) collective-permute-start(f32[4,128,128]{2,1,0:T(8,128)} %convolution_add_fusion.23), channel_id=1, source_target_pairs={{0,64},{64,128},{128,192},{192,256},{256,320},{320,384},{384,448},... | collective-permute-start | bytes 786440 | tf_op jit(solution)/shard_map/while/body/eval_jaxpr/ppermute | solution.py:25
  230.0 4.2 %collective-permute-done.1 = f32[4,128,128]{2,1,0:T(8,128)S(1)} collective-permute-done((f32[4,128,128]{2,1,0:T(8,128)}, f32[4,128,128]{2,1,0:T(8,128)S(1)}, u32[]{:S(2)}, u32[]{:S(2)}) %collective-permute-start.1) | collective-permute-done | bytes 262176 | tf_op jit(solution)/shard_map/while/body/eval_jaxpr/ppermute | solution.py:25
  235.3 4.9 %collective-permute-start = (f32[4,128,128]{2,1,0:T(8,128)}, f32[4,128,128]{2,1,0:T(8,128)S(1)}, u32[]{:S(2)}, u32[]{:S(2)}) collective-permute-start(f32[4,128,128]{2,1,0:T(8,128)} %convolution_add_fusion.23), channel_id=1, source_target_pairs={{0,64},{64,128},{128,192},{192,256},{256,320},{320,384},{384,448},... | collective-permute-start | bytes 786440 | tf_op jit(solution)/shard_map/while/body/eval_jaxpr/ppermute | solution.py:25
  243.2 4.2 %collective-permute-done.1 = f32[4,128,128]{2,1,0:T(8,128)S(1)} collective-permute-done((f32[4,128,128]{2,1,0:T(8,128)}, f32[4,128,128]{2,1,0:T(8,128)S(1)}, u32[]{:S(2)}, u32[]{:S(2)}) %collective-permute-start.1) | collective-permute-done | bytes 262176 | tf_op jit(solution)/shard_map/while/body/eval_jaxpr/ppermute | solution.py:25
  248.5 4.9 %collective-permute-start = (f32[4,128,128]{2,1,0:T(8,128)}, f32[4,128,128]{2,1,0:T(8,128)S(1)}, u32[]{:S(2)}, u32[]{:S(2)}) collective-permute-start(f32[4,128,128]{2,1,0:T(8,128)} %convolution_add_fusion.23), channel_id=1, source_target_pairs={{0,64},{64,128},{128,192},{192,256},{256,320},{320,384},{384,448},... | collective-permute-start | bytes 786440 | tf_op jit(solution)/shard_map/while/body/eval_jaxpr/ppermute | solution.py:25
  256.5 4.2 %collective-permute-done.1 = f32[4,128,128]{2,1,0:T(8,128)S(1)} collective-permute-done((f32[4,128,128]{2,1,0:T(8,128)}, f32[4,128,128]{2,1,0:T(8,128)S(1)}, u32[]{:S(2)}, u32[]{:S(2)}) %collective-permute-start.1) | collective-permute-done | bytes 262176 | tf_op jit(solution)/shard_map/while/body/eval_jaxpr/ppermute | solution.py:25
  263.0 9.8 %while.94 = (s32[]{:T(128)}, f32[4,128,128]{2,1,0:T(8,128)S(1)}, bf16[2,4,64,128]{3,2,1,0:T(8,128)(2,1)}, f32[2,4,128,128]{3,2,1,0:T(8,128)S(1)}, f32[2,4,1,1]{1...) while((s32[]{:T(128)}, f32[4,128,128]{2,1,0:T(8,128)S(1)}, ...), condition=%wide.region_12.14_spmd, body=%wide.region_11.13_spmd.sunk | while | flops 176357376 | bytes 4722913 | solution.py:80
  278.0 19.1 %while.95 = (s32[]{:T(128)}, f32[4,128,128]{2,1,0:T(8,128)S(1)}, f32[2,4,64,128]{3,2,1,0:T(8,128)}, f32[2,4,64,128]{3,2,1,0:T(8,128)}, f32[2,4,64,128]{3,2,0,1:T...) while((s32[]{:T(128)}, f32[4,128,128]{2,1,0:T(8,128)S(1)}, ...), condition=%wide.region_15.17_spmd, body=%wide.region_13.16_spmd.sunk | while | flops 352747520 | bytes 11543645 | solution.py:80
  322.9 18.2 %psum.28 = f32[4]{0:T(128)S(1)} all-reduce(f32[4]{0:T(128)S(1)} %negate_multiply_fusion), channel_id=1, replica_groups=mesh['seq_0'=8,'seq_1'=2,'dp_0'=8,'dp_1'=8] {'seq_0'}, use_global_device_ids=true, to_apply=%region_28.31 | all-reduce | flops 4 | bytes 32 | tf_op jit(solution)/shard_map/psum | solution.py:29
  341.1 2.5 psum.29
  343.5 17.0 %psum.30 = f32[4]{0:T(128)S(1)} all-reduce(f32[4]{0:T(128)S(1)} %psum.29), channel_id=1, replica_groups=mesh['seq_0'=8,'seq_1'=2,'dp_0'=8,'dp_1'=8] {'dp_0'}, use_global_device_ids=true, to_apply=%region_30.33 | all-reduce | flops 4 | bytes 32 | tf_op jit(solution)/shard_map/psum | solution.py:29
  360.5 30.0 %psum.31 = f32[4]{0:T(128)} all-reduce(f32[4]{0:T(128)S(1)} %psum.30), channel_id=1, replica_groups=mesh['seq_0'=8,'seq_1'=2,'dp_0'=8,'dp_1'=8] {'dp_1'}, use_global_device_ids=true, to_apply=%region_31.34 | all-reduce | flops 4 | bytes 32 | tf_op jit(solution)/shard_map/psum | solution.py:29
  (380 shorter events, 140.3 us)
Async XLA Ops:
  0.7 1.3 copy-start.53
  0.7 4.3 %copy-start.24 = (bf16[1,128,512]{2,1,0:T(8,128)(2,1)S(1)}, bf16[1,128,512]{2,1,0:T(8,128)(2,1)}, u32[]{:S(2)}) copy-start(bf16[1,128,512]{2,1,0:T(8,128)(2,1)} %param.26) | copy-start | bytes 393220
  4.1 45.2 %copy-start.43 = (f32[4,2,64]{2,1,0:T(2,128)}, f32[4,2,64]{2,1,0:T(2,128)S(1)}, u32[]{:S(2)}) copy-start(f32[4,2,64]{2,1,0:T(2,128)S(1)} %get-tuple-element.1063) | copy-start | bytes 6148
  6.1 51.5 %copy-start.35 = (f32[2,64,4]{1,0,2:T(2,128)}, f32[2,64,4]{1,0,2:T(2,128)S(1)}, u32[]{:S(2)}) copy-start(f32[2,64,4]{1,0,2:T(2,128)S(1)} %copy.325) | copy-start | bytes 6148
  54.3 3.1 copy-start.1
  57.6 1.3 copy-start.18
  63.4 1.0 copy-start
  65.5 7.9 %collective-permute-start = (f32[4,128,128]{2,1,0:T(8,128)}, f32[4,128,128]{2,1,0:T(8,128)S(1)}, u32[]{:S(2)}, u32[]{:S(2)}) collective-permute-start(f32[4,128,128]{2,1,0:T(8,128)} %convolution_add_fusion.23), channel_id=1, source_target_pairs={{0,64},{64,128},{128,192},{192,256},{256,320},{320,384},{384,448},... | collective-permute-start | bytes 786440 | tf_op jit(solution)/shard_map/while/body/eval_jaxpr/ppermute | solution.py:25
  68.5 7.8 %collective-permute-start.1 = (f32[4,128,128]{2,1,0:T(8,128)}, f32[4,128,128]{2,1,0:T(8,128)S(1)}, u32[]{:S(2)}, u32[]{:S(2)}) collective-permute-start(f32[4,128,128]{2,1,0:T(8,128)} %convolution_add_fusion.24), channel_id=1, source_target_pairs={{64,0},{128,64},{192,128},{256,192},{320,256},{384,320},{448,384},... | collective-permute-start | bytes 786440 | tf_op jit(solution)/shard_map/while/body/eval_jaxpr/ppermute | solution.py:25
  77.4 14.0 %collective-permute-start = (f32[4,128,128]{2,1,0:T(8,128)}, f32[4,128,128]{2,1,0:T(8,128)S(1)}, u32[]{:S(2)}, u32[]{:S(2)}) collective-permute-start(f32[4,128,128]{2,1,0:T(8,128)} %convolution_add_fusion.23), channel_id=1, source_target_pairs={{0,64},{64,128},{128,192},{192,256},{256,320},{320,384},{384,448},... | collective-permute-start | bytes 786440 | tf_op jit(solution)/shard_map/while/body/eval_jaxpr/ppermute | solution.py:25
  82.3 12.1 %collective-permute-start.1 = (f32[4,128,128]{2,1,0:T(8,128)}, f32[4,128,128]{2,1,0:T(8,128)S(1)}, u32[]{:S(2)}, u32[]{:S(2)}) collective-permute-start(f32[4,128,128]{2,1,0:T(8,128)} %convolution_add_fusion.24), channel_id=1, source_target_pairs={{64,0},{128,64},{192,128},{256,192},{320,256},{384,320},{448,384},... | collective-permute-start | bytes 786440 | tf_op jit(solution)/shard_map/while/body/eval_jaxpr/ppermute | solution.py:25
  95.6 8.0 %collective-permute-start = (f32[4,128,128]{2,1,0:T(8,128)}, f32[4,128,128]{2,1,0:T(8,128)S(1)}, u32[]{:S(2)}, u32[]{:S(2)}) collective-permute-start(f32[4,128,128]{2,1,0:T(8,128)} %convolution_add_fusion.23), channel_id=1, source_target_pairs={{0,64},{64,128},{128,192},{192,256},{256,320},{320,384},{384,448},... | collective-permute-start | bytes 786440 | tf_op jit(solution)/shard_map/while/body/eval_jaxpr/ppermute | solution.py:25
  98.6 7.9 %collective-permute-start.1 = (f32[4,128,128]{2,1,0:T(8,128)}, f32[4,128,128]{2,1,0:T(8,128)S(1)}, u32[]{:S(2)}, u32[]{:S(2)}) collective-permute-start(f32[4,128,128]{2,1,0:T(8,128)} %convolution_add_fusion.24), channel_id=1, source_target_pairs={{64,0},{128,64},{192,128},{256,192},{320,256},{384,320},{448,384},... | collective-permute-start | bytes 786440 | tf_op jit(solution)/shard_map/while/body/eval_jaxpr/ppermute | solution.py:25
  107.6 8.0 %collective-permute-start = (f32[4,128,128]{2,1,0:T(8,128)}, f32[4,128,128]{2,1,0:T(8,128)S(1)}, u32[]{:S(2)}, u32[]{:S(2)}) collective-permute-start(f32[4,128,128]{2,1,0:T(8,128)} %convolution_add_fusion.23), channel_id=1, source_target_pairs={{0,64},{64,128},{128,192},{192,256},{256,320},{320,384},{384,448},... | collective-permute-start | bytes 786440 | tf_op jit(solution)/shard_map/while/body/eval_jaxpr/ppermute | solution.py:25
  110.6 7.9 %collective-permute-start.1 = (f32[4,128,128]{2,1,0:T(8,128)}, f32[4,128,128]{2,1,0:T(8,128)S(1)}, u32[]{:S(2)}, u32[]{:S(2)}) collective-permute-start(f32[4,128,128]{2,1,0:T(8,128)} %convolution_add_fusion.24), channel_id=1, source_target_pairs={{64,0},{128,64},{192,128},{256,192},{320,256},{384,320},{448,384},... | collective-permute-start | bytes 786440 | tf_op jit(solution)/shard_map/while/body/eval_jaxpr/ppermute | solution.py:25
  119.6 8.0 %collective-permute-start = (f32[4,128,128]{2,1,0:T(8,128)}, f32[4,128,128]{2,1,0:T(8,128)S(1)}, u32[]{:S(2)}, u32[]{:S(2)}) collective-permute-start(f32[4,128,128]{2,1,0:T(8,128)} %convolution_add_fusion.23), channel_id=1, source_target_pairs={{0,64},{64,128},{128,192},{192,256},{256,320},{320,384},{384,448},... | collective-permute-start | bytes 786440 | tf_op jit(solution)/shard_map/while/body/eval_jaxpr/ppermute | solution.py:25
  122.6 7.9 %collective-permute-start.1 = (f32[4,128,128]{2,1,0:T(8,128)}, f32[4,128,128]{2,1,0:T(8,128)S(1)}, u32[]{:S(2)}, u32[]{:S(2)}) collective-permute-start(f32[4,128,128]{2,1,0:T(8,128)} %convolution_add_fusion.24), channel_id=1, source_target_pairs={{64,0},{128,64},{192,128},{256,192},{320,256},{384,320},{448,384},... | collective-permute-start | bytes 786440 | tf_op jit(solution)/shard_map/while/body/eval_jaxpr/ppermute | solution.py:25
  131.6 8.0 %collective-permute-start = (f32[4,128,128]{2,1,0:T(8,128)}, f32[4,128,128]{2,1,0:T(8,128)S(1)}, u32[]{:S(2)}, u32[]{:S(2)}) collective-permute-start(f32[4,128,128]{2,1,0:T(8,128)} %convolution_add_fusion.23), channel_id=1, source_target_pairs={{0,64},{64,128},{128,192},{192,256},{256,320},{320,384},{384,448},... | collective-permute-start | bytes 786440 | tf_op jit(solution)/shard_map/while/body/eval_jaxpr/ppermute | solution.py:25
  135.4 7.2 %collective-permute-start.1 = (f32[4,128,128]{2,1,0:T(8,128)}, f32[4,128,128]{2,1,0:T(8,128)S(1)}, u32[]{:S(2)}, u32[]{:S(2)}) collective-permute-start(f32[4,128,128]{2,1,0:T(8,128)} %convolution_add_fusion.24), channel_id=1, source_target_pairs={{64,0},{128,64},{192,128},{256,192},{320,256},{384,320},{448,384},... | collective-permute-start | bytes 786440 | tf_op jit(solution)/shard_map/while/body/eval_jaxpr/ppermute | solution.py:25
  143.7 8.0 %collective-permute-start = (f32[4,128,128]{2,1,0:T(8,128)}, f32[4,128,128]{2,1,0:T(8,128)S(1)}, u32[]{:S(2)}, u32[]{:S(2)}) collective-permute-start(f32[4,128,128]{2,1,0:T(8,128)} %convolution_add_fusion.23), channel_id=1, source_target_pairs={{0,64},{64,128},{128,192},{192,256},{256,320},{320,384},{384,448},... | collective-permute-start | bytes 786440 | tf_op jit(solution)/shard_map/while/body/eval_jaxpr/ppermute | solution.py:25
  148.6 6.1 %collective-permute-start.1 = (f32[4,128,128]{2,1,0:T(8,128)}, f32[4,128,128]{2,1,0:T(8,128)S(1)}, u32[]{:S(2)}, u32[]{:S(2)}) collective-permute-start(f32[4,128,128]{2,1,0:T(8,128)} %convolution_add_fusion.24), channel_id=1, source_target_pairs={{64,0},{128,64},{192,128},{256,192},{320,256},{384,320},{448,384},... | collective-permute-start | bytes 786440 | tf_op jit(solution)/shard_map/while/body/eval_jaxpr/ppermute | solution.py:25
  155.8 8.0 %collective-permute-start = (f32[4,128,128]{2,1,0:T(8,128)}, f32[4,128,128]{2,1,0:T(8,128)S(1)}, u32[]{:S(2)}, u32[]{:S(2)}) collective-permute-start(f32[4,128,128]{2,1,0:T(8,128)} %convolution_add_fusion.23), channel_id=1, source_target_pairs={{0,64},{64,128},{128,192},{192,256},{256,320},{320,384},{384,448},... | collective-permute-start | bytes 786440 | tf_op jit(solution)/shard_map/while/body/eval_jaxpr/ppermute | solution.py:25
  161.9 6.1 %collective-permute-start.1 = (f32[4,128,128]{2,1,0:T(8,128)}, f32[4,128,128]{2,1,0:T(8,128)S(1)}, u32[]{:S(2)}, u32[]{:S(2)}) collective-permute-start(f32[4,128,128]{2,1,0:T(8,128)} %convolution_add_fusion.24), channel_id=1, source_target_pairs={{64,0},{128,64},{192,128},{256,192},{320,256},{384,320},{448,384},... | collective-permute-start | bytes 786440 | tf_op jit(solution)/shard_map/while/body/eval_jaxpr/ppermute | solution.py:25
  169.1 8.0 %collective-permute-start = (f32[4,128,128]{2,1,0:T(8,128)}, f32[4,128,128]{2,1,0:T(8,128)S(1)}, u32[]{:S(2)}, u32[]{:S(2)}) collective-permute-start(f32[4,128,128]{2,1,0:T(8,128)} %convolution_add_fusion.23), channel_id=1, source_target_pairs={{0,64},{64,128},{128,192},{192,256},{256,320},{320,384},{384,448},... | collective-permute-start | bytes 786440 | tf_op jit(solution)/shard_map/while/body/eval_jaxpr/ppermute | solution.py:25
  175.1 6.1 %collective-permute-start.1 = (f32[4,128,128]{2,1,0:T(8,128)}, f32[4,128,128]{2,1,0:T(8,128)S(1)}, u32[]{:S(2)}, u32[]{:S(2)}) collective-permute-start(f32[4,128,128]{2,1,0:T(8,128)} %convolution_add_fusion.24), channel_id=1, source_target_pairs={{64,0},{128,64},{192,128},{256,192},{320,256},{384,320},{448,384},... | collective-permute-start | bytes 786440 | tf_op jit(solution)/shard_map/while/body/eval_jaxpr/ppermute | solution.py:25
  182.3 8.0 %collective-permute-start = (f32[4,128,128]{2,1,0:T(8,128)}, f32[4,128,128]{2,1,0:T(8,128)S(1)}, u32[]{:S(2)}, u32[]{:S(2)}) collective-permute-start(f32[4,128,128]{2,1,0:T(8,128)} %convolution_add_fusion.23), channel_id=1, source_target_pairs={{0,64},{64,128},{128,192},{192,256},{256,320},{320,384},{384,448},... | collective-permute-start | bytes 786440 | tf_op jit(solution)/shard_map/while/body/eval_jaxpr/ppermute | solution.py:25
  188.3 6.1 %collective-permute-start.1 = (f32[4,128,128]{2,1,0:T(8,128)}, f32[4,128,128]{2,1,0:T(8,128)S(1)}, u32[]{:S(2)}, u32[]{:S(2)}) collective-permute-start(f32[4,128,128]{2,1,0:T(8,128)} %convolution_add_fusion.24), channel_id=1, source_target_pairs={{64,0},{128,64},{192,128},{256,192},{320,256},{384,320},{448,384},... | collective-permute-start | bytes 786440 | tf_op jit(solution)/shard_map/while/body/eval_jaxpr/ppermute | solution.py:25
  195.6 8.0 %collective-permute-start = (f32[4,128,128]{2,1,0:T(8,128)}, f32[4,128,128]{2,1,0:T(8,128)S(1)}, u32[]{:S(2)}, u32[]{:S(2)}) collective-permute-start(f32[4,128,128]{2,1,0:T(8,128)} %convolution_add_fusion.23), channel_id=1, source_target_pairs={{0,64},{64,128},{128,192},{192,256},{256,320},{320,384},{384,448},... | collective-permute-start | bytes 786440 | tf_op jit(solution)/shard_map/while/body/eval_jaxpr/ppermute | solution.py:25
  201.6 6.1 %collective-permute-start.1 = (f32[4,128,128]{2,1,0:T(8,128)}, f32[4,128,128]{2,1,0:T(8,128)S(1)}, u32[]{:S(2)}, u32[]{:S(2)}) collective-permute-start(f32[4,128,128]{2,1,0:T(8,128)} %convolution_add_fusion.24), channel_id=1, source_target_pairs={{64,0},{128,64},{192,128},{256,192},{320,256},{384,320},{448,384},... | collective-permute-start | bytes 786440 | tf_op jit(solution)/shard_map/while/body/eval_jaxpr/ppermute | solution.py:25
  208.8 8.0 %collective-permute-start = (f32[4,128,128]{2,1,0:T(8,128)}, f32[4,128,128]{2,1,0:T(8,128)S(1)}, u32[]{:S(2)}, u32[]{:S(2)}) collective-permute-start(f32[4,128,128]{2,1,0:T(8,128)} %convolution_add_fusion.23), channel_id=1, source_target_pairs={{0,64},{64,128},{128,192},{192,256},{256,320},{320,384},{384,448},... | collective-permute-start | bytes 786440 | tf_op jit(solution)/shard_map/while/body/eval_jaxpr/ppermute | solution.py:25
  214.8 6.1 %collective-permute-start.1 = (f32[4,128,128]{2,1,0:T(8,128)}, f32[4,128,128]{2,1,0:T(8,128)S(1)}, u32[]{:S(2)}, u32[]{:S(2)}) collective-permute-start(f32[4,128,128]{2,1,0:T(8,128)} %convolution_add_fusion.24), channel_id=1, source_target_pairs={{64,0},{128,64},{192,128},{256,192},{320,256},{384,320},{448,384},... | collective-permute-start | bytes 786440 | tf_op jit(solution)/shard_map/while/body/eval_jaxpr/ppermute | solution.py:25
  222.0 8.0 %collective-permute-start = (f32[4,128,128]{2,1,0:T(8,128)}, f32[4,128,128]{2,1,0:T(8,128)S(1)}, u32[]{:S(2)}, u32[]{:S(2)}) collective-permute-start(f32[4,128,128]{2,1,0:T(8,128)} %convolution_add_fusion.23), channel_id=1, source_target_pairs={{0,64},{64,128},{128,192},{192,256},{256,320},{320,384},{384,448},... | collective-permute-start | bytes 786440 | tf_op jit(solution)/shard_map/while/body/eval_jaxpr/ppermute | solution.py:25
  228.1 6.1 %collective-permute-start.1 = (f32[4,128,128]{2,1,0:T(8,128)}, f32[4,128,128]{2,1,0:T(8,128)S(1)}, u32[]{:S(2)}, u32[]{:S(2)}) collective-permute-start(f32[4,128,128]{2,1,0:T(8,128)} %convolution_add_fusion.24), channel_id=1, source_target_pairs={{64,0},{128,64},{192,128},{256,192},{320,256},{384,320},{448,384},... | collective-permute-start | bytes 786440 | tf_op jit(solution)/shard_map/while/body/eval_jaxpr/ppermute | solution.py:25
  235.3 8.0 %collective-permute-start = (f32[4,128,128]{2,1,0:T(8,128)}, f32[4,128,128]{2,1,0:T(8,128)S(1)}, u32[]{:S(2)}, u32[]{:S(2)}) collective-permute-start(f32[4,128,128]{2,1,0:T(8,128)} %convolution_add_fusion.23), channel_id=1, source_target_pairs={{0,64},{64,128},{128,192},{192,256},{256,320},{320,384},{384,448},... | collective-permute-start | bytes 786440 | tf_op jit(solution)/shard_map/while/body/eval_jaxpr/ppermute | solution.py:25
  241.3 6.1 %collective-permute-start.1 = (f32[4,128,128]{2,1,0:T(8,128)}, f32[4,128,128]{2,1,0:T(8,128)S(1)}, u32[]{:S(2)}, u32[]{:S(2)}) collective-permute-start(f32[4,128,128]{2,1,0:T(8,128)} %convolution_add_fusion.24), channel_id=1, source_target_pairs={{64,0},{128,64},{192,128},{256,192},{320,256},{384,320},{448,384},... | collective-permute-start | bytes 786440 | tf_op jit(solution)/shard_map/while/body/eval_jaxpr/ppermute | solution.py:25
  248.5 8.0 %collective-permute-start = (f32[4,128,128]{2,1,0:T(8,128)}, f32[4,128,128]{2,1,0:T(8,128)S(1)}, u32[]{:S(2)}, u32[]{:S(2)}) collective-permute-start(f32[4,128,128]{2,1,0:T(8,128)} %convolution_add_fusion.23), channel_id=1, source_target_pairs={{0,64},{64,128},{128,192},{192,256},{256,320},{320,384},{384,448},... | collective-permute-start | bytes 786440 | tf_op jit(solution)/shard_map/while/body/eval_jaxpr/ppermute | solution.py:25
  254.5 6.1 %collective-permute-start.1 = (f32[4,128,128]{2,1,0:T(8,128)}, f32[4,128,128]{2,1,0:T(8,128)S(1)}, u32[]{:S(2)}, u32[]{:S(2)}) collective-permute-start(f32[4,128,128]{2,1,0:T(8,128)} %convolution_add_fusion.24), channel_id=1, source_target_pairs={{64,0},{128,64},{192,128},{256,192},{320,256},{384,320},{448,384},... | collective-permute-start | bytes 786440 | tf_op jit(solution)/shard_map/while/body/eval_jaxpr/ppermute | solution.py:25
  265.3 1.4 copy-start.34
  267.9 1.0 copy-start.4
  270.1 1.4 copy-start.34
  282.4 1.0 copy-start.11
  291.9 1.0 copy-start.11
  297.1 1.6 copy-start.41
  299.6 1.0 copy-start.26
  299.6 1.0 copy-start.38
  300.7 1.5 copy-start.16
  302.9 1.0 copy-start.17
  303.5 2.8 copy-start.45
  (61 other events, 47.0 us)
where the time goes:
time: 393 us; the launch traced here: 391 us
  starting transfers between devices  99.9 us (25%)
  blocking collectives  67.7 us (17%)
  matrix products  63.8 us (16%)
  waiting for transfers between devices  62.7 us (16%)
  other arithmetic  49.4 us (13%)
  local copies, waits for them, and re-layouts  44.4 us (11%)
    ppermute x30, starting transfers between devices, passed_along(): lax.ppermute(value, axis, [(source, source + steps) for source in range(f...  99.9 us
    psum x4, blocking collectives, by_axis(): return functools.reduce(lax.psum, axes, x)  67.7 us
    ppermute x30, waiting for transfers between devices, passed_along(): lax.ppermute(value, axis, [(source, source + steps) for source in range(f...  62.7 us
    another operation x5, other arithmetic, recurrence(): jax.scipy.linalg.solve_triangular(system, beta_b[..., None] * value_b, lo...  39.6 us
    unnamed x110, local copies, waits for them, and re-layouts  17.7 us
    dot_general x15, matrix products, paired_turn(): jnp.einsum('hij,hjk->hik', transfer, carried[0], precision=highest) + offset  16.7 us
    dot_general x15, matrix products, paired_turn(): jnp.einsum('hij,hjk->hik', adjoint_map, carried[1], precision=highest)  16.6 us
    while x52, local copies, waits for them, and re-layouts  11.9 us
  transfers between devices with their start and end apart: 30, of which 22 were waited for; matrix products, arithmetic and copies ran while one was open for 4% of the time, Pallas kernels for 0%

commit v1 on v0

v1 whole, which is shorter than its diff:
```python
import functools

import jax
import jax.numpy as jnp
from jax import lax
from jax.experimental import pallas as pl
from jax.experimental.pallas import tpu as pltpu
from jax.sharding import Mesh
from jax.sharding import PartitionSpec as P

H = 4
D = 128
C = 128
EPSILON = 1e-06
ROWS = 32
MESH = pl.DeviceIdType.MESH
f32 = jnp.float32
bf16 = jnp.bfloat16


def mm(a, b):
    return lax.dot_general(a, b, (((1,), (0,)), ((), ())), preferred_element_type=f32)


def mm_t(a, b):
    return lax.dot_general(a, b, (((1,), (1,)), ((), ())), preferred_element_type=f32)


def split(x):
    high = x.astype(bf16)
    return high, (x - high.astype(f32)).astype(bf16)


def split3(x):
    high, rest = x.astype(bf16), None
    rest = x - high.astype(f32)
    mid = rest.astype(bf16)
    return high, mid, (rest - mid.astype(f32)).astype(bf16)


def wide(x):
    return jnp.concatenate(split(x), axis=1)


def tall2(x):
    return jnp.concatenate([x, x], axis=0)


def fold(x):
    half = x.shape[1] // 2
    return x[:, :half] + x[:, half:]


def right(b):
    return tall2(wide(b))


def right_t(b):
    high, low = split(b)
    return jnp.concatenate(
        [jnp.concatenate([high, high], axis=1), jnp.concatenate([low, low], axis=1)], axis=0
    )


def rows_of(x):
    return jnp.sum(x, axis=1, keepdims=True)


def kernel(
    sizes,
    q_ref, k_ref, v_ref, alpha_ref, beta_ref, rate_ref, do_ref,
    o_ref, dq_ref, dk_ref, dv_ref, dalpha_ref, dbeta_ref, drate_ref,
    tbc, exch, chip_t, chip_tt, chip_b, chip_c,
    fin, fout, bin_, bout, sends, sendd, s0, ds1,
    keep_u, keep_pu, keep_y0, keep_ew, keep_f1,
    ar_seq, ar_x, ar_z, ar_own,
    exch_send, exch_recv, f_send, f_recv, b_send, b_recv, s_send, s_recv, d_send, d_recv,
    seq_send, seq_recv, x_send, x_recv, z_send, z_recv,
):
    ny, nx, nz = sizes
    y = lax.axis_index("y")
    c = lax.axis_index("c")
    ix = lax.axis_index("x")
    iz = lax.axis_index("z")
    nseq = 2 * ny
    me = 2 * y + c
    other = 1 - c

    barrier = pltpu.get_barrier_semaphore()
    for step in range(1, nseq):
        peer = lax.rem(me + step, nseq)
        pl.semaphore_signal(barrier, inc=1, device_id={"y": peer // 2, "c": lax.rem(peer, 2)}, device_id_type=MESH)
    for step in range(1, nx):
        pl.semaphore_signal(barrier, inc=1, device_id={"x": lax.rem(ix + step, nx)}, device_id_type=MESH)
    for step in range(1, nz):
        pl.semaphore_signal(barrier, inc=1, device_id={"z": lax.rem(iz + step, nz)}, device_id_type=MESH)

    heads = range(H)
    row = lax.broadcasted_iota(jnp.int32, (C, C), 0)
    col = lax.broadcasted_iota(jnp.int32, (C, C), 1)
    lower = row >= col
    strict = row > col
    upper = row <= col
    strict_upper = row < col
    eye = jnp.where(row == col, 1.0, 0.0).astype(f32)

    def part(ref, h):
        return ref[:, h * D:(h + 1) * D]

    alpha = alpha_ref[...]
    beta = beta_ref[...]
    head_row = lax.broadcasted_iota(jnp.int32, (H, C), 0)
    rate = jnp.zeros((H, C), f32)
    for h in heads:
        rate = jnp.where(head_row == h, rate_ref[h], rate)
    rate = jnp.exp(rate)
    soft = jnp.maximum(alpha, 0.0) + jnp.log1p(jnp.exp(-jnp.abs(alpha)))
    log_gate = -rate * soft
    bounded = jnp.maximum(log_gate, -120.0)
    tri_up = jnp.where(upper, 1.0, 0.0).astype(bf16)
    summed = mm(jnp.concatenate(split3(bounded), axis=0), tri_up)
    g_rows = summed[:H] + summed[H:2 * H] + summed[2 * H:]
    stacked = jnp.concatenate([g_rows, beta], axis=0)
    columns = jnp.transpose(jnp.concatenate([stacked, jnp.zeros((C - 2 * H, C), f32)], axis=0))

    g_r = [g_rows[h:h + 1, :] for h in heads]
    b_r = [beta[h:h + 1, :] for h in heads]
    g_c = [columns[:, h:h + 1] for h in heads]
    b_c = [columns[:, H + h:H + h + 1] for h in heads]
    g_end = [g_rows[h:h + 1, C - 1:C] for h in heads]
    gamma = [jnp.exp(g_end[h]) for h in heads]
    grow_c = [jnp.exp(g_c[h]) for h in heads]
    grow_r = [jnp.exp(g_r[h]) for h in heads]
    end_c = [jnp.exp(g_end[h] - g_c[h]) for h in heads]

    gram = []
    for h in heads:
        both = jnp.concatenate([part(k_ref, h), part(q_ref, h)], axis=0)
        gram.append(mm_t(both, both))
    rk_c, rk_r, rq_c, rq_r = [], [], [], []
    for h in heads:
        kk = gram[h][:C, :C] * eye
        qq = gram[h][C:, C:] * eye
        rk_c.append(lax.rsqrt(rows_of(kk) + EPSILON))
        rk_r.append(lax.rsqrt(jnp.sum(kk, axis=0, keepdims=True) + EPSILON))
        rq_c.append(lax.rsqrt(rows_of(qq) + EPSILON))
        rq_r.append(lax.rsqrt(jnp.sum(qq, axis=0, keepdims=True) + EPSILON))

    def decay(h):
        return jnp.exp(jnp.where(lower, g_c[h] - g_r[h], -1e30))

    def decay_t(h):
        return jnp.exp(jnp.where(upper, g_r[h] - g_c[h], -1e30))

    a_mat, p_mat, pt_mat = [], [], []
    for h in heads:
        fall = decay(h)
        scaled = fall * rk_r[h]
        a_mat.append(jnp.where(strict, gram[h][:C, :C] * scaled * (b_c[h] * rk_c[h]), 0.0))
        p_mat.append(gram[h][C:, :C] * scaled * rq_c[h])
        pt_mat.append(gram[h][:C, C:] * (decay_t(h) * rq_r[h]) * rk_c[h])

    same16 = (row // 16) == (col // 16)
    same64 = (row // 64) == (col // 64)
    power, inv = [], []
    for h in heads:
        a16 = jnp.where(same16, a_mat[h], 0.0)
        inv.append(eye - a16)
        power.append(fold(mm(wide(a16), right(a16))))
    for level in range(2):
        for h in heads:
            both = fold(mm(jnp.concatenate([wide(inv[h]), wide(power[h])], axis=0), right(power[h])))
            inv[h] = inv[h] + both[:C]
            power[h] = both[C:]
    for h in heads:
        inv[h] = inv[h] + fold(mm(wide(inv[h]), right(power[h])))
    step_mat = []
    for h in heads:
        off = jnp.where(same64, jnp.where(same16, 0.0, a_mat[h]), 0.0)
        step_mat.append(fold(mm(wide(inv[h]), right(off))))
    square = []
    for h in heads:
        both = mm(wide(step_mat[h]), jnp.concatenate([right(inv[h]), right(step_mat[h])], axis=1))
        inv[h] = inv[h] - fold(both[:, :2 * C])
        square.append(fold(both[:, 2 * C:]))
    for h in heads:
        inv[h] = inv[h] + fold(mm(wide(square[h]), right(inv[h])))
    for h in heads:
        off = jnp.where(same64, 0.0, a_mat[h])
        step_mat[h] = fold(mm(wide(inv[h]), right(off)))
    for h in heads:
        inv[h] = inv[h] - fold(mm(wide(step_mat[h]), right(inv[h])))

    u_mat, w_mat = [], []
    for h in heads:
        key, value = part(k_ref, h), part(v_ref, h)
        u_mat.append(mm(wide(inv[h] * b_r[h]), tall2(value)))
        w_mat.append(mm(wide(inv[h] * (b_r[h] * grow_r[h] * rk_r[h])), tall2(key)))
    for h in heads:
        scale = end_c[h] * rk_c[h]
        key_t = jnp.transpose(part(k_ref, h))
        tb = mm(key_t, jnp.concatenate([wide(w_mat[h] * scale), wide(u_mat[h] * scale)], axis=1))
        tbc[h, 0] = gamma[h] * eye - fold(tb[:, :2 * D])
        tbc[h, 1] = jnp.transpose(fold(tb[:, 2 * D:]))
    for h in heads:
        pwu = mm(wide(p_mat[h]), jnp.concatenate([right(w_mat[h]), right(u_mat[h])], axis=1))
        keep_pu[h] = fold(pwu[:, 2 * D:])
        keep_u[h] = u_mat[h]
        e1 = part(q_ref, h).astype(f32) * (rq_c[h] * grow_c[h]) - fold(pwu[:, :2 * D])
        keep_ew[h, :C] = wide(e1)
        keep_ew[h, C:] = wide(w_mat[h])
        tbc[h, 2] = fold(mm(jnp.transpose(part(do_ref, h)), wide(e1)))

    pl.semaphore_wait(barrier, nseq - 1 + nx - 1 + nz - 1)

    def swap(hh):
        return pltpu.make_async_remote_copy(
            src_ref=tbc.at[2 * other + hh], dst_ref=exch.at[hh],
            send_sem=exch_send.at[hh], recv_sem=exch_recv.at[hh],
            device_id={"c": other}, device_id_type=MESH,
        )

    for hh in range(2):
        swap(hh).start()

    for h in heads:
        z = mm(wide(pt_mat[h]), tall2(part(do_ref, h)))
        inv_t = wide(jnp.transpose(inv[h]))
        key_end = part(k_ref, h).astype(f32) * (end_c[h] * rk_c[h])
        both = mm(inv_t, jnp.concatenate([right(z), right(key_end)], axis=1))
        keep_y0[h] = fold(both[:, :2 * D])
        keep_f1[h] = wide(fold(both[:, 2 * D:]))

    first = c == 0
    for hh in range(2):
        swap(hh).wait()

    def pair(hh, item):
        mine, theirs = tbc[2 * c + hh, item], exch[hh, item]
        return jnp.where(first, mine, theirs), jnp.where(first, theirs, mine)

    for hh in range(2):
        t0, t1 = pair(hh, 0)
        b0, b1 = pair(hh, 1)
        c0, c1 = pair(hh, 2)
        both = fold(mm(jnp.concatenate([wide(t1), wide(c1)], axis=0), right(t0)))
        whole = both[:D]
        chip_t[hh] = right(whole)
        chip_tt[hh] = right_t(whole)
        chip_b[hh] = fold(mm_t(wide(b0), right_t(t1))) + b1
        chip_c[hh] = both[D:] + c0

    chunks = [(hh, r) for hh in range(2) for r in range(0, D, ROWS)]

    def f_copy(i, source):
        hh, r = chunks[i]
        return pltpu.make_async_remote_copy(
            src_ref=source.at[hh, pl.ds(r, ROWS)], dst_ref=fin.at[hh, pl.ds(r, ROWS)],
            send_sem=f_send.at[i], recv_sem=f_recv.at[i],
            device_id={"y": lax.rem(y + 1, ny)}, device_id_type=MESH,
        )

    def b_copy(i, source):
        hh, r = chunks[i]
        return pltpu.make_async_remote_copy(
            src_ref=source.at[hh, pl.ds(r, ROWS)], dst_ref=bin_.at[hh, pl.ds(r, ROWS)],
            send_sem=b_send.at[i], recv_sem=b_recv.at[i],
            device_id={"y": lax.rem(y + ny - 1, ny)}, device_id_type=MESH,
        )

    def s_copy(hh):
        return pltpu.make_async_remote_copy(
            src_ref=sends.at[hh], dst_ref=s0.at[2 * c + hh],
            send_sem=s_send.at[hh], recv_sem=s_recv.at[hh],
            device_id={"c": other}, device_id_type=MESH,
        )

    def d_copy(hh):
        return pltpu.make_async_remote_copy(
            src_ref=sendd.at[hh], dst_ref=ds1.at[2 * c + hh],
            send_sem=d_send.at[hh], recv_sem=d_recv.at[hh],
            device_id={"c": other}, device_id_type=MESH,
        )

    def forward():
        @pl.when(y == 0)
        def _():
            for i in range(len(chunks)):
                f_copy(i, chip_b).start()
            fin[...] = jnp.zeros_like(fin)

        @pl.when(y > 0)
        def _():
            for i, (hh, r) in enumerate(chunks):
                f_copy(i, fout).wait_recv()

                @pl.when(y < ny - 1)
                def _():
                    here = pl.ds(r, ROWS)
                    fout[hh, here] = fold(mm_t(wide(fin[hh, here]), chip_tt[hh])) + chip_b[hh, here]
                    f_copy(i, fout).start()

        for hh in range(2):
            t0, _ = pair(hh, 0)
            b0, _ = pair(hh, 1)
            start = fin[hh]
            middle = fold(mm_t(wide(start), right_t(t0))) + b0
            s0[2 * c + hh] = jnp.where(first, start, middle)
            sends[hh] = jnp.where(first, middle, start)
            s_copy(hh).start()

    def backward():
        @pl.when(y == ny - 1)
        def _():
            for i in range(len(chunks)):
                b_copy(i, chip_c).start()
            bin_[...] = jnp.zeros_like(bin_)

        @pl.when(y < ny - 1)
        def _():
            for i, (hh, r) in enumerate(chunks):
                b_copy(i, bout).wait_recv()

                @pl.when(y > 0)
                def _():
                    here = pl.ds(r, ROWS)
                    bout[hh, here] = fold(mm(wide(bin_[hh, here]), chip_t[hh])) + chip_c[hh, here]
                    b_copy(i, bout).start()

        for hh in range(2):
            _, t1 = pair(hh, 0)
            _, c1 = pair(hh, 2)
            end = bin_[hh]
            middle = fold(mm(wide(end), right(t1))) + c1
            ds1[2 * c + hh] = jnp.where(first, middle, end)
            sendd[hh] = jnp.where(first, end, middle)
            d_copy(hh).start()

    @pl.when(y < ny // 2)
    def _():
        forward()
        backward()

    @pl.when(y >= ny // 2)
    def _():
        backward()
        forward()

    for hh in range(2):
        s_copy(hh).wait()
        d_copy(hh).wait()

    @pl.when(y < ny - 1)
    def _():
        for i in range(len(chunks)):
            f_copy(i, fout).wait_send()

    @pl.when(y > 0)
    def _():
        for i in range(len(chunks)):
            b_copy(i, bout).wait_send()

    d_mat, y_mat, start_w, end_w, dot_s = [], [], [], [], []
    for h in heads:
        start, end = s0[h], ds1[h]
        start_w.append(start)
        end_w.append(end)
        dot_s.append(jnp.sum(jnp.sum(start * end, axis=0, keepdims=True), axis=1, keepdims=True))
        ew = fold(mm_t(keep_ew[h], right_t(start)))
        o_ref[:, h * D:(h + 1) * D] = (keep_pu[h] + ew[:C]).astype(bf16)
        d_mat.append(keep_u[h] - ew[C:])
        y_mat.append(keep_y0[h] + fold(mm_t(keep_f1[h], right_t(end))))
    lane = lax.broadcasted_iota(jnp.int32, (C, C), 1)
    gathered = jnp.zeros((C, C), f32)
    last = lax.broadcasted_iota(jnp.int32, (C, 1), 0) == C - 1
    for h in heads:
        key, query, value, cot = part(k_ref, h), part(q_ref, h), part(v_ref, h), part(do_ref, h)
        dm, ym = d_mat[h], y_mat[h]
        left = jnp.concatenate([jnp.concatenate([cot, jnp.zeros_like(cot)], axis=1), wide(ym)], axis=0)
        with_s = fold(mm(left, right(start_w[h])))
        with_d = fold(mm_t(left, right_t(dm)))
        y_high, y_low = split(ym)
        flipped = mm_t(
            wide(dm),
            jnp.concatenate([
                jnp.concatenate([cot, cot], axis=1),
                jnp.concatenate([y_high, y_high], axis=1),
                jnp.concatenate([y_low, y_low], axis=1),
            ], axis=0),
        )
        dds = fold(mm(wide(dm), right(end_w[h]))) * end_c[h]
        fall = decay(h) * rk_r[h]
        fall_t = decay_t(h)
        x_w = with_d[:C] * fall
        n_w = jnp.where(strict, with_d[C:] * fall, 0.0) * (-b_c[h])
        xn = mm(jnp.concatenate([wide(x_w), wide(n_w)], axis=0), tall2(key))
        xt = flipped[:, :C] * (fall_t * rq_r[h])
        nt = jnp.where(strict_upper, (flipped[:, C:2 * C] + flipped[:, 2 * C:]) * fall_t, 0.0) * (-b_r[h] * rk_r[h])
        dk_col = mm(jnp.concatenate([wide(nt), wide(xt)], axis=1), jnp.concatenate([tall2(key), tall2(query)], axis=0)) + dds
        dqn = with_s[:C] * grow_c[h] + xn[:C]
        dk_row = xn[C:] - with_s[C:] * (b_c[h] * grow_c[h])
        kn = key.astype(f32) * rk_c[h]
        qn = query.astype(f32) * rq_c[h]
        sum_q = rows_of(qn * dqn)
        sum_r = rows_of(kn * dk_row)
        sum_c = rows_of(kn * dk_col)
        sum_e = jnp.sum(rows_of(kn * dds), axis=0, keepdims=True)
        sum_v = rows_of(ym * value.astype(f32))
        dq_ref[:, h * D:(h + 1) * D] = ((dqn - qn * sum_q) * rq_c[h]).astype(bf16)
        dk_ref[:, h * D:(h + 1) * D] = ((dk_row + dk_col - kn * (sum_r + sum_c)) * rk_c[h]).astype(bf16)
        dv_ref[:, h * D:(h + 1) * D] = (ym * b_c[h]).astype(bf16)
        dbeta = sum_v + sum_r / b_c[h]
        dg = sum_q + sum_r - sum_c + jnp.where(last, sum_e + gamma[h] * dot_s[h], 0.0)
        gathered = jnp.where(lane == h, dg, gathered)
        gathered = jnp.where(lane == H + h, dbeta, gathered)
    as_rows = jnp.transpose(gathered)
    dbeta_ref[...] = as_rows[H:2 * H]
    tri_low = jnp.where(lower, 1.0, 0.0).astype(bf16)
    back = mm(jnp.concatenate(split3(as_rows[:H]), axis=0), tri_low)
    dlog = back[:H] + back[H:2 * H] + back[2 * H:]
    dalpha_ref[...] = dlog * -rate * jax.nn.sigmoid(alpha)
    own = jnp.concatenate([dlog * log_gate, jnp.zeros((8 - H, C), f32)], axis=0)

    def stage(total, slot, count, buf, send, recv, device):
        ar_own[slot] = total
        if count == 1:
            return total
        index = {0: me, 1: ix, 2: iz}[slot]

        def copy(step):
            return pltpu.make_async_remote_copy(
                src_ref=ar_own.at[slot], dst_ref=buf.at[index],
                send_sem=send.at[step], recv_sem=recv.at[step],
                device_id=device(lax.rem(index + step, count)), device_id_type=MESH,
            )

        for step in range(1, count):
            copy(step).start()
        buf[index] = total
        for step in range(1, count):
            copy(step).wait()
        result = buf[0]
        for j in range(1, count):
            result = result + buf[j]
        return result

    total = stage(own, 0, nseq, ar_seq, seq_send, seq_recv, lambda p: {"y": p // 2, "c": lax.rem(p, 2)})
    total = stage(total, 1, nx, ar_x, x_send, x_recv, lambda p: {"x": p})
    total = stage(total, 2, nz, ar_z, z_send, z_recv, lambda p: {"z": p})
    for h in heads:
        drate_ref[h] = jnp.sum(total[h:h + 1, :])


def local(sizes, queries, keys, values, alpha, beta, log_rate, grad_out):
    ny, nx, nz = sizes
    vmem = pl.BlockSpec(memory_space=pltpu.VMEM)
    smem = pl.BlockSpec(memory_space=pltpu.SMEM)
    wide_out = jax.ShapeDtypeStruct((C, H * D), bf16)
    gate_out = jax.ShapeDtypeStruct((H, C), f32)
    chunk_count = 2 * (D // ROWS)
    dma = pltpu.SemaphoreType.DMA
    square = (D, D)
    outs = pl.pallas_call(
        functools.partial(kernel, sizes),
        name="delta_rule",
        out_shape=(wide_out, wide_out, wide_out, wide_out, gate_out, gate_out, jax.ShapeDtypeStruct((H,), f32)),
        in_specs=[vmem, vmem, vmem, vmem, vmem, smem, vmem],
        out_specs=(vmem, vmem, vmem, vmem, vmem, vmem, smem),
        scratch_shapes=[
            pltpu.VMEM((H, 3) + square, f32),
            pltpu.VMEM((2, 3) + square, f32),
            pltpu.VMEM((2, 2 * D, 2 * D), bf16),
            pltpu.VMEM((2, 2 * D, 2 * D), bf16),
            pltpu.VMEM((2,) + square, f32),
            pltpu.VMEM((2,) + square, f32),
            pltpu.VMEM((2,) + square, f32),
            pltpu.VMEM((2,) + square, f32),
            pltpu.VMEM((2,) + square, f32),
            pltpu.VMEM((2,) + square, f32),
            pltpu.VMEM((2,) + square, f32),
            pltpu.VMEM((2,) + square, f32),
            pltpu.VMEM((H,) + square, f32),
            pltpu.VMEM((H,) + square, f32),
            pltpu.VMEM((H,) + square, f32),
            pltpu.VMEM((H,) + square, f32),
            pltpu.VMEM((H,) + square, f32),
            pltpu.VMEM((H, 2 * C, 2 * D), bf16),
            pltpu.VMEM((H, C, 2 * D), bf16),
            pltpu.VMEM((2 * ny, 8, C), f32),
            pltpu.VMEM((nx, 8, C), f32),
            pltpu.VMEM((nz, 8, C), f32),
            pltpu.VMEM((3, 8, C), f32),
            dma((2,)), dma((2,)),
            dma((chunk_count,)), dma((chunk_count,)),
            dma((chunk_count,)), dma((chunk_count,)),
            dma((2,)), dma((2,)), dma((2,)), dma((2,)),
            dma((2 * ny,)), dma((2 * ny,)),
            dma((nx,)), dma((nx,)), dma((nz,)), dma((nz,)),
        ],
        compiler_params=pltpu.CompilerParams(collective_id=0, has_side_effects=True),
    )(
        queries[0], keys[0], values[0],
        jnp.swapaxes(alpha[0], 0, 1), jnp.swapaxes(beta[0], 0, 1), log_rate, grad_out[0],
    )
    return (
        outs[0][None], outs[1][None], outs[2][None], outs[3][None],
        jnp.swapaxes(outs[4], 0, 1)[None], jnp.swapaxes(outs[5], 0, 1)[None], outs[6],
    )


def build(devices, ny, nx, nz):
    axes = Mesh(devices.reshape(ny, 2, nx, nz), ("y", "c", "x", "z"))
    rows = P(("x", "z"), ("y", "c"), None)
    return jax.shard_map(
        functools.partial(local, (ny, nx, nz)),
        mesh=axes,
        in_specs=(rows, rows, rows, rows, rows, P(), rows),
        out_specs=(rows, rows, rows, rows, rows, rows, P()),
        check_vma=False,
    )


def solution(mesh):
    return build(mesh.devices, 8, 8, 8)
```

time: 393 us -> 73 us (0.19)
  starting transfers between devices: 99.9 us -> 0 us
  blocking collectives: 67.7 us -> 0 us
  Pallas kernels: 0 us -> 66.1 us
  matrix products: 63.8 us -> 0 us
  waiting for transfers between devices: 62.7 us -> 0 us
  other arithmetic: 49.4 us -> 0 us
  local copies, waits for them, and re-layouts: 44.4 us -> 5.98 us
    ppermute x30 -> x0, starting transfers between devices: 99.9 us -> none  [passed_along(): lax.ppermute(value, axis, [(source, source + steps) for source in range(f...]
    psum x4 -> x0, blocking collectives: 67.7 us -> none  [by_axis(): return functools.reduce(lax.psum, axes, x)]
    pallas_call x0 -> x1, Pallas kernels: none -> 66.1 us  [local(): pl.pallas_call(functools.partial(kernel, sizes), name='delta_rule', out_s...]
    ppermute x30 -> x0, waiting for transfers between devices: 62.7 us -> none  [passed_along(): lax.ppermute(value, axis, [(source, source + steps) for source in range(f...]
    dot_general x74 -> x0, matrix products: 58.8 us -> none  [the longest x15 16.7 us: paired_turn(): jnp.einsum('hij,hjk->hik', transfer, carried[0], precision=highest) + offset]
    another operation x7 -> x0, other arithmetic: 42.3 us -> none  [the longest x5 39.6 us: recurrence(): jax.scipy.linalg.solve_triangular(system, beta_b[..., None] * value_b, lo...]
    while x54 -> x0, local copies, waits for them, and re-layouts: 11.9 us -> none
    unnamed x110 -> x19, local copies, waits for them, and re-layouts: 17.7 us -> 5.98 us
  transfers between devices with their start and end apart: 30 -> 0, of which waited for: 22 -> 0; matrix products, arithmetic and copies ran while one was open for 4% -> 0% of each run, Pallas kernels for 0% -> 0%
where the time goes in v1:
time: 73 us; the launch traced here: 72.7 us
  Pallas kernels  66.1 us (91%)
  local copies, waits for them, and re-layouts  5.98 us (8%)
    pallas_call x1, Pallas kernels, local(): pl.pallas_call(functools.partial(kernel, sizes), name='delta_rule', out_s...  66.1 us
    unnamed x19, local copies, waits for them, and re-layouts  5.98 us

profile of v1, /device:TPU:16, one launch (start us, length us, event | category | flops | bytes accessed | tf_op | source)
XLA Modules:
  0.0 72.7 jit_solution(8156029859834028754)
XLA Ops:
  0.6 66.1 %delta_rule.1 = (bf16[128,512]{1,0:T(8,128)(2,1)}, bf16[128,512]{1,0:T(8,128)(2,1)}, bf16[128,512]{1,0:T(8,128)(2,1)}, bf16[128,512]{1,0:T(8,128)(2,1)}, f32[4,1...) custom-call(bf16[128,512]{1,0:T(8,128)(2,1)} %bitcast.20, bf16[128,512]{1,0:T(8,128)(2,1)} %bitcast.21, ...), custom_call_target="tpu_custom_call" | custom-call | tf_op jit(solution)/shard_map/delta_rule/pallas_call | solution.py:463
  66.7 0.0 copy-start.2
  66.7 1.6 %copy.21 = bf16[1,128,512]{2,1,0:T(8,128)(2,1)} copy(bf16[1,128,512]{2,1,0:T(8,128)(2,1)} %bitcast.27) | data formatting | bytes 262144
  68.3 0.0 copy-done.2
  68.3 0.0 copy-start.1
  68.4 0.7 copy.22
  69.0 0.3 copy-done.1
  69.3 0.0 copy-start
  69.3 0.7 copy.23
  70.0 0.3 copy-done
  70.3 0.0 copy-start.4
  70.3 0.7 copy.24
  70.9 0.0 copy-done.4
  70.9 0.0 copy-start.3
  70.9 0.6 copy.25
  71.5 0.1 copy-done.3
  71.6 0.0 copy-start.5
  71.6 0.6 copy.26
  72.1 0.1 copy-done.5
  72.2 0.5 copy.27
Async XLA Ops:
  66.7 1.6 %copy-start.2 = (bf16[128,512]{1,0:T(8,128)(2,1)S(1)}, bf16[128,512]{1,0:T(8,128)(2,1)}, u32[]{:S(2)}) copy-start(bf16[128,512]{1,0:T(8,128)(2,1)} %get-tuple-element.15) | copy-start | bytes 393220
  68.3 1.0 %copy-start.1 = (bf16[128,512]{1,0:T(8,128)(2,1)S(1)}, bf16[128,512]{1,0:T(8,128)(2,1)}, u32[]{:S(2)}) copy-start(bf16[128,512]{1,0:T(8,128)(2,1)} %get-tuple-element.16) | copy-start | bytes 393220
  69.3 1.0 %copy-start = (bf16[128,512]{1,0:T(8,128)(2,1)S(1)}, bf16[128,512]{1,0:T(8,128)(2,1)}, u32[]{:S(2)}) copy-start(bf16[128,512]{1,0:T(8,128)(2,1)} %get-tuple-element.17) | copy-start | bytes 393220
  70.3 0.7 copy-start.4
  70.9 0.6 copy-start.3
  71.6 0.7 copy-start.5

commit v2 on v1

--- a/solution.py
+++ b/solution.py
@@ -72,7 +72,7 @@
     o_ref, dq_ref, dk_ref, dv_ref, dalpha_ref, dbeta_ref, drate_ref,
     tbc, exch, chip_t, chip_tt, chip_b, chip_c,
     fin, fout, bin_, bout, sends, sendd, s0, ds1,
-    keep_u, keep_pu, keep_y0, keep_ew, keep_f1,
+    keep_u, keep_pu, keep_y0, keep_ew, keep_f1, keep_pa,
     ar_seq, ar_x, ar_z, ar_own,
     exch_send, exch_recv, f_send, f_recv, b_send, b_recv, s_send, s_recv, d_send, d_recv,
     seq_send, seq_recv, x_send, x_recv, z_send, z_recv,
@@ -251,6 +251,7 @@
         chip_c[hh] = both[D:] + c0
 
     chunks = [(hh, r) for hh in range(2) for r in range(0, D, ROWS)]
+    per_head = D // ROWS
 
     def f_copy(i, source):
         hh, r = chunks[i]
@@ -282,59 +283,80 @@
             device_id={"c": other}, device_id_type=MESH,
         )
 
+    @pl.when(y == 0)
+    def _():
+        for i in range(len(chunks)):
+            f_copy(i, chip_b).start()
+
+    @pl.when(y == ny - 1)
+    def _():
+        for i in range(len(chunks)):
+            b_copy(i, chip_c).start()
+
+    for h in heads:
+        between = g_c[h] - g_r[h]
+        keep_pa[h, :C] = wide(jnp.where(lower, p_mat[h] * between, 0.0))
+        keep_pa[h, C:] = wide(jnp.where(strict, a_mat[h] * between, 0.0))
+
+    def last_forward(hh):
+        t0, _ = pair(hh, 0)
+        b0, _ = pair(hh, 1)
+        start = fin[hh]
+        middle = fold(mm_t(wide(start), right_t(t0))) + b0
+        s0[2 * c + hh] = jnp.where(first, start, middle)
+        sends[hh] = jnp.where(first, middle, start)
+        s_copy(hh).start()
+
+    def last_backward(hh):
+        _, t1 = pair(hh, 0)
+        _, c1 = pair(hh, 2)
+        end = bin_[hh]
+        middle = fold(mm(wide(end), right(t1))) + c1
+        ds1[2 * c + hh] = jnp.where(first, middle, end)
+        sendd[hh] = jnp.where(first, end, middle)
+        d_copy(hh).start()
+
     def forward():
         @pl.when(y == 0)
         def _():
-            for i in range(len(chunks)):
-                f_copy(i, chip_b).start()
             fin[...] = jnp.zeros_like(fin)
 
-        @pl.when(y > 0)
+        @pl.when(jnp.logical_and(y > 0, y < ny - 1))
         def _():
             for i, (hh, r) in enumerate(chunks):
+                here = pl.ds(r, ROWS)
                 f_copy(i, fout).wait_recv()
-
-                @pl.when(y < ny - 1)
-                def _():
-                    here = pl.ds(r, ROWS)
-                    fout[hh, here] = fold(mm_t(wide(fin[hh, here]), chip_tt[hh])) + chip_b[hh, here]
-                    f_copy(i, fout).start()
+                fout[hh, here] = fold(mm_t(wide(fin[hh, here]), chip_tt[hh])) + chip_b[hh, here]
+                f_copy(i, fout).start()
 
         for hh in range(2):
-            t0, _ = pair(hh, 0)
-            b0, _ = pair(hh, 1)
-            start = fin[hh]
-            middle = fold(mm_t(wide(start), right_t(t0))) + b0
-            s0[2 * c + hh] = jnp.where(first, start, middle)
-            sends[hh] = jnp.where(first, middle, start)
-            s_copy(hh).start()
+            @pl.when(y == ny - 1)
+            def _():
+                for i in range(hh * per_head, (hh + 1) * per_head):
+                    f_copy(i, fout).wait_recv()
+
+            last_forward(hh)
 
     def backward():
         @pl.when(y == ny - 1)
         def _():
-            for i in range(len(chunks)):
-                b_copy(i, chip_c).start()
             bin_[...] = jnp.zeros_like(bin_)
 
-        @pl.when(y < ny - 1)
+        @pl.when(jnp.logical_and(y > 0, y < ny - 1))
         def _():
             for i, (hh, r) in enumerate(chunks):
+                here = pl.ds(r, ROWS)
                 b_copy(i, bout).wait_recv()
-
-                @pl.when(y > 0)
-                def _():
-                    here = pl.ds(r, ROWS)
-                    bout[hh, here] = fold(mm(wide(bin_[hh, here]), chip_t[hh])) + chip_c[hh, here]
-                    b_copy(i, bout).start()
+                bout[hh, here] = fold(mm(wide(bin_[hh, here]), chip_t[hh])) + chip_c[hh, here]
+                b_copy(i, bout).start()
 
         for hh in range(2):
-            _, t1 = pair(hh, 0)
-            _, c1 = pair(hh, 2)
-            end = bin_[hh]
-            middle = fold(mm(wide(end), right(t1))) + c1
-            ds1[2 * c + hh] = jnp.where(first, middle, end)
-            sendd[hh] = jnp.where(first, end, middle)
-            d_copy(hh).start()
+            @pl.when(y == 0)
+            def _():
+                for i in range(hh * per_head, (hh + 1) * per_head):
+                    b_copy(i, bout).wait_recv()
+
+            last_backward(hh)
 
     @pl.when(y < ny // 2)
     def _():
@@ -360,24 +382,68 @@
         for i in range(len(chunks)):
             b_copy(i, bout).wait_send()
 
-    d_mat, y_mat, start_w, end_w, dot_s = [], [], [], [], []
+    groups = (
+        (me, nseq, ar_seq, seq_send, seq_recv, lambda p: {"y": p // 2, "c": lax.rem(p, 2)}),
+        (ix, nx, ar_x, x_send, x_recv, lambda p: {"x": p}),
+        (iz, nz, ar_z, z_send, z_recv, lambda p: {"z": p}),
+    )
+
+    def part_copy(slot, step):
+        index, count, buf, send, recv, device = groups[slot]
+        return pltpu.make_async_remote_copy(
+            src_ref=ar_own.at[slot], dst_ref=buf.at[index],
+            send_sem=send.at[step], recv_sem=recv.at[step],
+            device_id=device(lax.rem(index + step, count)), device_id_type=MESH,
+        )
+
+    def sum_start(slot, total):
+        index, count, buf = groups[slot][:3]
+        ar_own[slot] = total
+        for step in range(1, count):
+            part_copy(slot, step).start()
+        buf[index] = total
+
+    def sum_finish(slot):
+        _, count, buf = groups[slot][:3]
+        for step in range(1, count):
+            part_copy(slot, step).wait()
+        result = buf[0]
+        for j in range(1, count):
+            result = result + buf[j]
+        return result
+
+    d_mat, y_mat, dds_mat, dot_s, rate_rows = [], [], [], [], []
     for h in heads:
         start, end = s0[h], ds1[h]
-        start_w.append(start)
-        end_w.append(end)
-        dot_s.append(jnp.sum(jnp.sum(start * end, axis=0, keepdims=True), axis=1, keepdims=True))
         ew = fold(mm_t(keep_ew[h], right_t(start)))
         o_ref[:, h * D:(h + 1) * D] = (keep_pu[h] + ew[:C]).astype(bf16)
         d_mat.append(keep_u[h] - ew[C:])
         y_mat.append(keep_y0[h] + fold(mm_t(keep_f1[h], right_t(end))))
+        dot_s.append(jnp.sum(start * end, axis=0, keepdims=True))
+    for h in heads:
+        key, query, cot = part(k_ref, h), part(q_ref, h), part(do_ref, h)
+        high, low = split(s0[h])
+        raw = fold(mm_t(jnp.concatenate([query, key], axis=0), jnp.concatenate([high, low], axis=0)))
+        dm_right = right(d_mat[h])
+        scored = fold(mm(keep_pa[h], dm_right))
+        dds = fold(mm(wide(d_mat[h]), right(ds1[h]))) * end_c[h]
+        dds_mat.append(dds)
+        gated = g_c[h] * grow_c[h]
+        terms = cot.astype(f32) * (scored[:C] + raw[:C] * (gated * rq_c[h]))
+        terms = terms - y_mat[h] * (scored[C:] + raw[C:] * (gated * b_c[h] * rk_c[h]))
+        terms = terms + (key.astype(f32) * dds) * ((g_end[h] - g_c[h]) * rk_c[h])
+        rate_rows.append(jnp.sum(terms, axis=0, keepdims=True) + (g_end[h] * gamma[h]) * dot_s[h])
+    own = jnp.concatenate(rate_rows + [jnp.zeros((8 - H, C), f32)], axis=0)
+    sum_start(0, own)
+
     lane = lax.broadcasted_iota(jnp.int32, (C, C), 1)
-    gathered = jnp.zeros((C, C), f32)
     last = lax.broadcasted_iota(jnp.int32, (C, 1), 0) == C - 1
-    for h in heads:
+
+    def gradients(h):
         key, query, value, cot = part(k_ref, h), part(q_ref, h), part(v_ref, h), part(do_ref, h)
-        dm, ym = d_mat[h], y_mat[h]
+        dm, ym, dds = d_mat[h], y_mat[h], dds_mat[h]
         left = jnp.concatenate([jnp.concatenate([cot, jnp.zeros_like(cot)], axis=1), wide(ym)], axis=0)
-        with_s = fold(mm(left, right(start_w[h])))
+        with_s = fold(mm(left, right(s0[h])))
         with_d = fold(mm_t(left, right_t(dm)))
         y_high, y_low = split(ym)
         flipped = mm_t(
@@ -388,7 +454,6 @@
                 jnp.concatenate([y_low, y_low], axis=1),
             ], axis=0),
         )
-        dds = fold(mm(wide(dm), right(end_w[h]))) * end_c[h]
         fall = decay(h) * rk_r[h]
         fall_t = decay_t(h)
         x_w = with_d[:C] * fall
@@ -410,45 +475,43 @@
         dk_ref[:, h * D:(h + 1) * D] = ((dk_row + dk_col - kn * (sum_r + sum_c)) * rk_c[h]).astype(bf16)
         dv_ref[:, h * D:(h + 1) * D] = (ym * b_c[h]).astype(bf16)
         dbeta = sum_v + sum_r / b_c[h]
-        dg = sum_q + sum_r - sum_c + jnp.where(last, sum_e + gamma[h] * dot_s[h], 0.0)
+        dg = sum_q + sum_r - sum_c + jnp.where(last, sum_e + gamma[h] * rows_of(dot_s[h]), 0.0)
+        return dg, dbeta
+
+    gathered = jnp.zeros((C, C), f32)
+
+    def place(gathered, h):
+        dg, dbeta = gradients(h)
         gathered = jnp.where(lane == h, dg, gathered)
-        gathered = jnp.where(lane == H + h, dbeta, gathered)
+        return jnp.where(lane == H + h, dbeta, gathered)
+
+    for h in range(H // 2):
+        gathered = place(gathered, h)
+    sum_start(1, sum_finish(0))
+    for h in range(H // 2, H):
+        gathered = place(gathered, h)
+    sum_start(2, sum_finish(1))
     as_rows = jnp.transpose(gathered)
     dbeta_ref[...] = as_rows[H:2 * H]
     tri_low = jnp.where(lower, 1.0, 0.0).astype(bf16)
     back = mm(jnp.concatenate(split3(as_rows[:H]), axis=0), tri_low)
     dlog = back[:H] + back[H:2 * H] + back[2 * H:]
     dalpha_ref[...] = dlog * -rate * jax.nn.sigmoid(alpha)
-    own = jnp.concatenate([dlog * log_gate, jnp.zeros((8 - H, C), f32)], axis=0)
-
-    def stage(total, slot, count, buf, send, recv, device):
-        ar_own[slot] = total
-        if count == 1:
-            return total
-        index = {0: me, 1: ix, 2: iz}[slot]
-
-        def copy(step):
-            return pltpu.make_async_remote_copy(
-                src_ref=ar_own.at[slot], dst_ref=buf.at[index],
-                send_sem=send.at[step], recv_sem=recv.at[step],
-                device_id=device(lax.rem(index + step, count)), device_id_type=MESH,
-            )
-
-        for step in range(1, count):
-            copy(step).start()
-        buf[index] = total
-        for step in range(1, count):
-            copy(step).wait()
-        result = buf[0]
-        for j in range(1, count):
-            result = result + buf[j]
-        return result
-
-    total = stage(own, 0, nseq, ar_seq, seq_send, seq_recv, lambda p: {"y": p // 2, "c": lax.rem(p, 2)})
-    total = stage(total, 1, nx, ar_x, x_send, x_recv, lambda p: {"x": p})
-    total = stage(total, 2, nz, ar_z, z_send, z_recv, lambda p: {"z": p})
+    total = sum_finish(2)
     for h in heads:
         drate_ref[h] = jnp.sum(total[h:h + 1, :])
+
+
+def deliver(*refs):
+    count = 6
+    ins, rate_in, outs, rate_out, sem = refs[:count], refs[count], refs[count + 1:2 * count + 1], refs[-2], refs[-1]
+    copies = [pltpu.make_async_copy(ins[i], outs[i], sem.at[i]) for i in range(count)]
+    for copy in copies:
+        copy.start()
+    for h in range(H):
+        rate_out[h] = rate_in[h]
+    for copy in copies:
+        copy.wait()
 
 
 def local(sizes, queries, keys, values, alpha, beta, log_rate, grad_out):
@@ -460,10 +523,11 @@
     chunk_count = 2 * (D // ROWS)
     dma = pltpu.SemaphoreType.DMA
     square = (D, D)
+    shapes = (wide_out, wide_out, wide_out, wide_out, gate_out, gate_out, jax.ShapeDtypeStruct((H,), f32))
     outs = pl.pallas_call(
         functools.partial(kernel, sizes),
         name="delta_rule",
-        out_shape=(wide_out, wide_out, wide_out, wide_out, gate_out, gate_out, jax.ShapeDtypeStruct((H,), f32)),
+        out_shape=shapes,
         in_specs=[vmem, vmem, vmem, vmem, vmem, smem, vmem],
         out_specs=(vmem, vmem, vmem, vmem, vmem, vmem, smem),
         scratch_shapes=[
@@ -486,6 +550,7 @@
             pltpu.VMEM((H,) + square, f32),
             pltpu.VMEM((H, 2 * C, 2 * D), bf16),
             pltpu.VMEM((H, C, 2 * D), bf16),
+            pltpu.VMEM((H, 2 * C, 2 * C), bf16),
             pltpu.VMEM((2 * ny, 8, C), f32),
             pltpu.VMEM((nx, 8, C), f32),
             pltpu.VMEM((nz, 8, C), f32),
@@ -502,6 +567,14 @@
         queries[0], keys[0], values[0],
         jnp.swapaxes(alpha[0], 0, 1), jnp.swapaxes(beta[0], 0, 1), log_rate, grad_out[0],
     )
+    outs = pl.pallas_call(
+        deliver,
+        name="deliver",
+        out_shape=shapes,
+        in_specs=[vmem] * 6 + [smem],
+        out_specs=tuple([pl.BlockSpec(memory_space=pl.ANY)] * 6 + [smem]),
+        scratch_shapes=[dma((6,))],
+    )(*outs)
     return (
         outs[0][None], outs[1][None], outs[2][None], outs[3][None],
         jnp.swapaxes(outs[4], 0, 1)[None], jnp.swapaxes(outs[5], 0, 1)[None], outs[6],

time: 73 us -> 68.3 us (0.936)
  local copies, waits for them, and re-layouts: 5.98 us -> 0 us
  Pallas kernels: 66.1 us -> 67.4 us
    unnamed x19 -> x0, local copies, waits for them, and re-layouts: 5.98 us -> none
    pallas_call x0 -> x1, Pallas kernels: none -> 2.47 us  [local(): pl.pallas_call(deliver, name='deliver', out_shape=shapes, in_specs=[vmem]...]
    pallas_call x1, Pallas kernels: 66.1 us -> 65 us  [local(): pl.pallas_call(functools.partial(kernel, sizes), name='delta_rule', out_s...]
where the time goes in v2:
time: 68.3 us; the launch traced here: 68.1 us
  Pallas kernels  67.4 us (99%)
    pallas_call x1, Pallas kernels, local(): pl.pallas_call(functools.partial(kernel, sizes), name='delta_rule', out_s...  65 us
    pallas_call x1, Pallas kernels, local(): pl.pallas_call(deliver, name='deliver', out_shape=shapes, in_specs=[vmem]...  2.47 us

profile of v2, /device:TPU:16, one launch (start us, length us, event | category | flops | bytes accessed | tf_op | source)
XLA Modules:
  0.0 68.1 jit_solution(4710881121868743709)
XLA Ops:
  0.6 65.0 %delta_rule.1 = (bf16[128,512]{1,0:T(8,128)(2,1)}, bf16[128,512]{1,0:T(8,128)(2,1)}, bf16[128,512]{1,0:T(8,128)(2,1)}, bf16[128,512]{1,0:T(8,128)(2,1)}, f32[4,1...) custom-call(bf16[128,512]{1,0:T(8,128)(2,1)} %bitcast.20, bf16[128,512]{1,0:T(8,128)(2,1)} %bitcast.21, ...), custom_call_target="tpu_custom_call" | custom-call | tf_op jit(solution)/shard_map/delta_rule/pallas_call | solution.py:527
  65.6 2.5 %deliver.1 = (bf16[128,512]{1,0:T(8,128)(2,1)}, bf16[128,512]{1,0:T(8,128)(2,1)}, bf16[128,512]{1,0:T(8,128)(2,1)}, bf16[128,512]{1,0:T(8,128)(2,1)}, f32[4,128]...) custom-call(bf16[128,512]{1,0:T(8,128)(2,1)} %get-tuple-element.21.refs_0_, bf16[128,512]{1,0:T(8,128)(2,1)} %get-tuple-element.22.refs_1_, ...), custom_call_target="tpu_custom_call" | custom-call | tf_op jit(solution)/shard_map/deliver/pallas_call | solution.py:570

commit v3 on v2

--- a/solution.py
+++ b/solution.py
@@ -152,13 +152,12 @@
     def decay_t(h):
         return jnp.exp(jnp.where(upper, g_r[h] - g_c[h], -1e30))
 
-    a_mat, p_mat, pt_mat = [], [], []
+    a_mat, p_mat = [], []
     for h in heads:
         fall = decay(h)
         scaled = fall * rk_r[h]
         a_mat.append(jnp.where(strict, gram[h][:C, :C] * scaled * (b_c[h] * rk_c[h]), 0.0))
         p_mat.append(gram[h][C:, :C] * scaled * rq_c[h])
-        pt_mat.append(gram[h][:C, C:] * (decay_t(h) * rq_r[h]) * rk_c[h])
 
     same16 = (row // 16) == (col // 16)
     same64 = (row // 64) == (col // 64)
@@ -203,10 +202,8 @@
         tbc[h, 0] = gamma[h] * eye - fold(tb[:, :2 * D])
         tbc[h, 1] = jnp.transpose(fold(tb[:, 2 * D:]))
     for h in heads:
-        pwu = mm(wide(p_mat[h]), jnp.concatenate([right(w_mat[h]), right(u_mat[h])], axis=1))
-        keep_pu[h] = fold(pwu[:, 2 * D:])
-        keep_u[h] = u_mat[h]
-        e1 = part(q_ref, h).astype(f32) * (rq_c[h] * grow_c[h]) - fold(pwu[:, :2 * D])
+        pw = fold(mm(wide(p_mat[h]), right(w_mat[h])))
+        e1 = part(q_ref, h).astype(f32) * (rq_c[h] * grow_c[h]) - pw
         keep_ew[h, :C] = wide(e1)
         keep_ew[h, C:] = wide(w_mat[h])
         tbc[h, 2] = fold(mm(jnp.transpose(part(do_ref, h)), wide(e1)))
@@ -216,7 +213,7 @@
     def swap(hh):
         return pltpu.make_async_remote_copy(
             src_ref=tbc.at[2 * other + hh], dst_ref=exch.at[hh],
-            send_sem=exch_send.at[hh], recv_sem=exch_recv.at[hh],
+            send_sem=exch_send.at[0], recv_sem=exch_recv.at[hh],
             device_id={"c": other}, device_id_type=MESH,
         )
 
@@ -224,7 +221,10 @@
         swap(hh).start()
 
     for h in heads:
-        z = mm(wide(pt_mat[h]), tall2(part(do_ref, h)))
+        keep_u[h] = u_mat[h]
+        keep_pu[h] = fold(mm(wide(p_mat[h]), right(u_mat[h])))
+        pt_mat = gram[h][:C, C:] * (decay_t(h) * rq_r[h]) * rk_c[h]
+        z = mm(wide(pt_mat), tall2(part(do_ref, h)))
         inv_t = wide(jnp.transpose(inv[h]))
         key_end = part(k_ref, h).astype(f32) * (end_c[h] * rk_c[h])
         both = mm(inv_t, jnp.concatenate([right(z), right(key_end)], axis=1))
@@ -232,66 +232,67 @@
         keep_f1[h] = wide(fold(both[:, 2 * D:]))
 
     first = c == 0
-    for hh in range(2):
-        swap(hh).wait()
+    chunks = [(hh, r) for hh in range(2) for r in range(0, D, ROWS)]
+    per_head = D // ROWS
+
+    def f_copy(i, source):
+        hh, r = chunks[i]
+        return pltpu.make_async_remote_copy(
+            src_ref=source.at[hh, pl.ds(r, ROWS)], dst_ref=fin.at[hh, pl.ds(r, ROWS)],
+            send_sem=f_send.at[0], recv_sem=f_recv.at[i],
+            device_id={"y": lax.rem(y + 1, ny)}, device_id_type=MESH,
+        )
+
+    def b_copy(i, source):
+        hh, r = chunks[i]
+        return pltpu.make_async_remote_copy(
+            src_ref=source.at[hh, pl.ds(r, ROWS)], dst_ref=bin_.at[hh, pl.ds(r, ROWS)],
+            send_sem=b_send.at[0], recv_sem=b_recv.at[i],
+            device_id={"y": lax.rem(y + ny - 1, ny)}, device_id_type=MESH,
+        )
+
+    def s_copy(hh):
+        return pltpu.make_async_remote_copy(
+            src_ref=sends.at[hh], dst_ref=s0.at[2 * c + hh],
+            send_sem=s_send.at[0], recv_sem=s_recv.at[0],
+            device_id={"c": other}, device_id_type=MESH,
+        )
+
+    def d_copy(hh):
+        return pltpu.make_async_remote_copy(
+            src_ref=sendd.at[hh], dst_ref=ds1.at[2 * c + hh],
+            send_sem=d_send.at[0], recv_sem=d_recv.at[0],
+            device_id={"c": other}, device_id_type=MESH,
+        )
+
+    first = c == 0
 
     def pair(hh, item):
         mine, theirs = tbc[2 * c + hh, item], exch[hh, item]
         return jnp.where(first, mine, theirs), jnp.where(first, theirs, mine)
 
     for hh in range(2):
+        swap(hh).wait_recv()
         t0, t1 = pair(hh, 0)
         b0, b1 = pair(hh, 1)
         c0, c1 = pair(hh, 2)
         both = fold(mm(jnp.concatenate([wide(t1), wide(c1)], axis=0), right(t0)))
         whole = both[:D]
+        chip_b[hh] = fold(mm_t(wide(b0), right_t(t1))) + b1
+        chip_c[hh] = both[D:] + c0
+
+        @pl.when(y == 0)
+        def _():
+            for i in range(hh * per_head, (hh + 1) * per_head):
+                f_copy(i, chip_b).start()
+
+        @pl.when(y == ny - 1)
+        def _():
+            for i in range(hh * per_head, (hh + 1) * per_head):
+                b_copy(i, chip_c).start()
+
         chip_t[hh] = right(whole)
         chip_tt[hh] = right_t(whole)
-        chip_b[hh] = fold(mm_t(wide(b0), right_t(t1))) + b1
-        chip_c[hh] = both[D:] + c0
-
-    chunks = [(hh, r) for hh in range(2) for r in range(0, D, ROWS)]
-    per_head = D // ROWS
-
-    def f_copy(i, source):
-        hh, r = chunks[i]
-        return pltpu.make_async_remote_copy(
-            src_ref=source.at[hh, pl.ds(r, ROWS)], dst_ref=fin.at[hh, pl.ds(r, ROWS)],
-            send_sem=f_send.at[i], recv_sem=f_recv.at[i],
-            device_id={"y": lax.rem(y + 1, ny)}, device_id_type=MESH,
-        )
-
-    def b_copy(i, source):
-        hh, r = chunks[i]
-        return pltpu.make_async_remote_copy(
-            src_ref=source.at[hh, pl.ds(r, ROWS)], dst_ref=bin_.at[hh, pl.ds(r, ROWS)],
-            send_sem=b_send.at[i], recv_sem=b_recv.at[i],
-            device_id={"y": lax.rem(y + ny - 1, ny)}, device_id_type=MESH,
-        )
-
-    def s_copy(hh):
-        return pltpu.make_async_remote_copy(
-            src_ref=sends.at[hh], dst_ref=s0.at[2 * c + hh],
-            send_sem=s_send.at[hh], recv_sem=s_recv.at[hh],
-            device_id={"c": other}, device_id_type=MESH,
-        )
-
-    def d_copy(hh):
-        return pltpu.make_async_remote_copy(
-            src_ref=sendd.at[hh], dst_ref=ds1.at[2 * c + hh],
-            send_sem=d_send.at[hh], recv_sem=d_recv.at[hh],
-            device_id={"c": other}, device_id_type=MESH,
-        )
-
-    @pl.when(y == 0)
-    def _():
-        for i in range(len(chunks)):
-            f_copy(i, chip_b).start()
-
-    @pl.when(y == ny - 1)
-    def _():
-        for i in range(len(chunks)):
-            b_copy(i, chip_c).start()
 
     for h in heads:
         between = g_c[h] - g_r[h]
@@ -368,19 +369,20 @@
         backward()
         forward()
 
-    for hh in range(2):
-        s_copy(hh).wait()
-        d_copy(hh).wait()
-
-    @pl.when(y < ny - 1)
-    def _():
-        for i in range(len(chunks)):
-            f_copy(i, fout).wait_send()
-
-    @pl.when(y > 0)
-    def _():
-        for i in range(len(chunks)):
-            b_copy(i, bout).wait_send()
+    def all_sent(source, sem, to):
+        return pltpu.make_async_remote_copy(
+            src_ref=source, dst_ref=source, send_sem=sem.at[0], recv_sem=sem.at[0],
+            device_id=to, device_id_type=MESH,
+        )
+
+    def all_came(source, landing, sem):
+        return pltpu.make_async_remote_copy(
+            src_ref=source, dst_ref=landing, send_sem=sem.at[0], recv_sem=sem.at[0],
+            device_id={"c": other}, device_id_type=MESH,
+        )
+
+    all_came(sends, s0.at[pl.ds(2 * other, 2)], s_recv).wait_recv()
+    all_came(sendd, ds1.at[pl.ds(2 * other, 2)], d_recv).wait_recv()
 
     groups = (
         (me, nseq, ar_seq, seq_send, seq_recv, lambda p: {"y": p // 2, "c": lax.rem(p, 2)}),
@@ -392,7 +394,7 @@
         index, count, buf, send, recv, device = groups[slot]
         return pltpu.make_async_remote_copy(
             src_ref=ar_own.at[slot], dst_ref=buf.at[index],
-            send_sem=send.at[step], recv_sem=recv.at[step],
+            send_sem=send.at[0], recv_sem=recv.at[0],
             device_id=device(lax.rem(index + step, count)), device_id_type=MESH,
         )
 
@@ -403,10 +405,18 @@
             part_copy(slot, step).start()
         buf[index] = total
 
+    def came(slot):
+        index, count, buf, send, recv, device = groups[slot]
+        others = buf.at[pl.ds(0, count - 1)]
+        return pltpu.make_async_remote_copy(
+            src_ref=others, dst_ref=others, send_sem=send.at[0], recv_sem=recv.at[0],
+            device_id=device(lax.rem(index + 1, count)), device_id_type=MESH,
+        )
+
     def sum_finish(slot):
         _, count, buf = groups[slot][:3]
-        for step in range(1, count):
-            part_copy(slot, step).wait()
+        if count > 1:
+            came(slot).wait_recv()
         result = buf[0]
         for j in range(1, count):
             result = result + buf[j]
@@ -433,7 +443,10 @@
         terms = terms - y_mat[h] * (scored[C:] + raw[C:] * (gated * b_c[h] * rk_c[h]))
         terms = terms + (key.astype(f32) * dds) * ((g_end[h] - g_c[h]) * rk_c[h])
         rate_rows.append(jnp.sum(terms, axis=0, keepdims=True) + (g_end[h] * gamma[h]) * dot_s[h])
-    own = jnp.concatenate(rate_rows + [jnp.zeros((8 - H, C), f32)], axis=0)
+    lane_row = lax.broadcasted_iota(jnp.int32, (1, C), 1)
+    own = jnp.zeros((1, C), f32)
+    for h in heads:
+        own = jnp.where(lane_row == h, rows_of(rate_rows[h]), own)
     sum_start(0, own)
 
     lane = lax.broadcasted_iota(jnp.int32, (C, C), 1)
@@ -499,7 +512,23 @@
     dalpha_ref[...] = dlog * -rate * jax.nn.sigmoid(alpha)
     total = sum_finish(2)
     for h in heads:
-        drate_ref[h] = jnp.sum(total[h:h + 1, :])
+        drate_ref[h] = jnp.sum(jnp.where(lane_row == h, total, 0.0))
+
+    all_sent(tbc.at[pl.ds(0, 2)], exch_send, {"c": other}).wait_send()
+    all_sent(sends, s_send, {"c": other}).wait_send()
+    all_sent(sendd, d_send, {"c": other}).wait_send()
+
+    @pl.when(y < ny - 1)
+    def _():
+        all_sent(fout, f_send, {"y": lax.rem(y + 1, ny)}).wait_send()
+
+    @pl.when(y > 0)
+    def _():
+        all_sent(bout, b_send, {"y": lax.rem(y + ny - 1, ny)}).wait_send()
+
+    for slot in range(3):
+        if groups[slot][1] > 1:
+            came(slot).wait_send()
 
 
 def deliver(*refs):
@@ -551,16 +580,16 @@
             pltpu.VMEM((H, 2 * C, 2 * D), bf16),
             pltpu.VMEM((H, C, 2 * D), bf16),
             pltpu.VMEM((H, 2 * C, 2 * C), bf16),
-            pltpu.VMEM((2 * ny, 8, C), f32),
-            pltpu.VMEM((nx, 8, C), f32),
-            pltpu.VMEM((nz, 8, C), f32),
-            pltpu.VMEM((3, 8, C), f32),
-            dma((2,)), dma((2,)),
-            dma((chunk_count,)), dma((chunk_count,)),
-            dma((chunk_count,)), dma((chunk_count,)),
-            dma((2,)), dma((2,)), dma((2,)), dma((2,)),
-            dma((2 * ny,)), dma((2 * ny,)),
-            dma((nx,)), dma((nx,)), dma((nz,)), dma((nz,)),
+            pltpu.VMEM((2 * ny, 1, C), f32),
+            pltpu.VMEM((nx, 1, C), f32),
+            pltpu.VMEM((nz, 1, C), f32),
+            pltpu.VMEM((3, 1, C), f32),
+            dma((1,)), dma((2,)),
+            dma((1,)), dma((chunk_count,)),
+            dma((1,)), dma((chunk_count,)),
+            dma((1,)), dma((1,)), dma((1,)), dma((1,)),
+            dma((1,)), dma((1,)),
+            dma((1,)), dma((1,)), dma((1,)), dma((1,)),
         ],
         compiler_params=pltpu.CompilerParams(collective_id=0, has_side_effects=True),
     )(

time: 68.3 us -> 65.9 us (0.965)
  Pallas kernels: 67.4 us -> 65.1 us
    pallas_call x1, Pallas kernels: 65 us -> 62.6 us  [local(): pl.pallas_call(functools.partial(kernel, sizes), name='delta_rule', out_s...]
where the time goes in v3:
time: 65.9 us; the launch traced here: 65.8 us
  Pallas kernels  65.1 us (99%)
    pallas_call x1, Pallas kernels, local(): pl.pallas_call(functools.partial(kernel, sizes), name='delta_rule', out_s...  62.6 us
    pallas_call x1, Pallas kernels, local(): pl.pallas_call(deliver, name='deliver', out_shape=shapes, in_specs=[vmem]...  2.47 us

profile of v3, /device:TPU:16, one launch (start us, length us, event | category | flops | bytes accessed | tf_op | source)
XLA Modules:
  0.0 65.8 jit_solution(1533603131430704876)
XLA Ops:
  0.6 62.6 %delta_rule.1 = (bf16[128,512]{1,0:T(8,128)(2,1)}, bf16[128,512]{1,0:T(8,128)(2,1)}, bf16[128,512]{1,0:T(8,128)(2,1)}, bf16[128,512]{1,0:T(8,128)(2,1)}, f32[4,1...) custom-call(bf16[128,512]{1,0:T(8,128)(2,1)} %bitcast.20, bf16[128,512]{1,0:T(8,128)(2,1)} %bitcast.21, ...), custom_call_target="tpu_custom_call" | custom-call | tf_op jit(solution)/shard_map/delta_rule/pallas_call | solution.py:556
  63.3 2.5 %deliver.1 = (bf16[128,512]{1,0:T(8,128)(2,1)}, bf16[128,512]{1,0:T(8,128)(2,1)}, bf16[128,512]{1,0:T(8,128)(2,1)}, bf16[128,512]{1,0:T(8,128)(2,1)}, f32[4,128]...) custom-call(bf16[128,512]{1,0:T(8,128)(2,1)} %get-tuple-element.21.refs_0_, bf16[128,512]{1,0:T(8,128)(2,1)} %get-tuple-element.22.refs_1_, ...), custom_call_target="tpu_custom_call" | custom-call | tf_op jit(solution)/shard_map/deliver/pallas_call | solution.py:599

commit v4 on v3

--- a/solution.py
+++ b/solution.py
@@ -73,9 +73,9 @@
     tbc, exch, chip_t, chip_tt, chip_b, chip_c,
     fin, fout, bin_, bout, sends, sendd, s0, ds1,
     keep_u, keep_pu, keep_y0, keep_ew, keep_f1, keep_pa,
-    ar_seq, ar_x, ar_z, ar_own,
+    ar_seq, ar_plane, ar_own,
     exch_send, exch_recv, f_send, f_recv, b_send, b_recv, s_send, s_recv, d_send, d_recv,
-    seq_send, seq_recv, x_send, x_recv, z_send, z_recv,
+    seq_send, seq_recv, plane_send, plane_recv,
 ):
     ny, nx, nz = sizes
     y = lax.axis_index("y")
@@ -90,10 +90,15 @@
     for step in range(1, nseq):
         peer = lax.rem(me + step, nseq)
         pl.semaphore_signal(barrier, inc=1, device_id={"y": peer // 2, "c": lax.rem(peer, 2)}, device_id_type=MESH)
-    for step in range(1, nx):
-        pl.semaphore_signal(barrier, inc=1, device_id={"x": lax.rem(ix + step, nx)}, device_id_type=MESH)
-    for step in range(1, nz):
-        pl.semaphore_signal(barrier, inc=1, device_id={"z": lax.rem(iz + step, nz)}, device_id_type=MESH)
+    nplane = nx * nz
+    spot = ix * nz + iz
+
+    def greet(step, carry):
+        peer = lax.rem(spot + step, nplane)
+        pl.semaphore_signal(barrier, inc=1, device_id={"x": peer // nz, "z": lax.rem(peer, nz)}, device_id_type=MESH)
+        return carry
+
+    lax.fori_loop(1, nplane, greet, 0)
 
     heads = range(H)
     row = lax.broadcasted_iota(jnp.int32, (C, C), 0)
@@ -208,7 +213,7 @@
         keep_ew[h, C:] = wide(w_mat[h])
         tbc[h, 2] = fold(mm(jnp.transpose(part(do_ref, h)), wide(e1)))
 
-    pl.semaphore_wait(barrier, nseq - 1 + nx - 1 + nz - 1)
+    pl.semaphore_wait(barrier, nseq - 1 + nplane - 1)
 
     def swap(hh):
         return pltpu.make_async_remote_copy(
@@ -386,8 +391,7 @@
 
     groups = (
         (me, nseq, ar_seq, seq_send, seq_recv, lambda p: {"y": p // 2, "c": lax.rem(p, 2)}),
-        (ix, nx, ar_x, x_send, x_recv, lambda p: {"x": p}),
-        (iz, nz, ar_z, z_send, z_recv, lambda p: {"z": p}),
+        (spot, nplane, ar_plane, plane_send, plane_recv, lambda p: {"x": p // nz, "z": lax.rem(p, nz)}),
     )
 
     def part_copy(slot, step):
@@ -401,8 +405,12 @@
     def sum_start(slot, total):
         index, count, buf = groups[slot][:3]
         ar_own[slot] = total
-        for step in range(1, count):
+
+        def start(step, carry):
             part_copy(slot, step).start()
+            return carry
+
+        lax.fori_loop(1, count, start, 0)
         buf[index] = total
 
     def came(slot):
@@ -417,10 +425,7 @@
         _, count, buf = groups[slot][:3]
         if count > 1:
             came(slot).wait_recv()
-        result = buf[0]
-        for j in range(1, count):
-            result = result + buf[j]
-        return result
+        return jnp.sum(buf[...], axis=0)
 
     d_mat, y_mat, dds_mat, dot_s, rate_rows = [], [], [], [], []
     for h in heads:
@@ -498,19 +503,16 @@
         gathered = jnp.where(lane == h, dg, gathered)
         return jnp.where(lane == H + h, dbeta, gathered)
 
-    for h in range(H // 2):
+    for h in heads:
         gathered = place(gathered, h)
     sum_start(1, sum_finish(0))
-    for h in range(H // 2, H):
-        gathered = place(gathered, h)
-    sum_start(2, sum_finish(1))
     as_rows = jnp.transpose(gathered)
     dbeta_ref[...] = as_rows[H:2 * H]
     tri_low = jnp.where(lower, 1.0, 0.0).astype(bf16)
     back = mm(jnp.concatenate(split3(as_rows[:H]), axis=0), tri_low)
     dlog = back[:H] + back[H:2 * H] + back[2 * H:]
     dalpha_ref[...] = dlog * -rate * jax.nn.sigmoid(alpha)
-    total = sum_finish(2)
+    total = sum_finish(1)
     for h in heads:
         drate_ref[h] = jnp.sum(jnp.where(lane_row == h, total, 0.0))
 
@@ -526,7 +528,7 @@
     def _():
         all_sent(bout, b_send, {"y": lax.rem(y + ny - 1, ny)}).wait_send()
 
-    for slot in range(3):
+    for slot in range(2):
         if groups[slot][1] > 1:
             came(slot).wait_send()
 
@@ -581,15 +583,14 @@
             pltpu.VMEM((H, C, 2 * D), bf16),
             pltpu.VMEM((H, 2 * C, 2 * C), bf16),
             pltpu.VMEM((2 * ny, 1, C), f32),
-            pltpu.VMEM((nx, 1, C), f32),
-            pltpu.VMEM((nz, 1, C), f32),
-            pltpu.VMEM((3, 1, C), f32),
+            pltpu.VMEM((nx * nz, 1, C), f32),
+            pltpu.VMEM((2, 1, C), f32),
             dma((1,)), dma((2,)),
             dma((1,)), dma((chunk_count,)),
             dma((1,)), dma((chunk_count,)),
             dma((1,)), dma((1,)), dma((1,)), dma((1,)),
             dma((1,)), dma((1,)),
-            dma((1,)), dma((1,)), dma((1,)), dma((1,)),
+            dma((1,)), dma((1,)),
         ],
         compiler_params=pltpu.CompilerParams(collective_id=0, has_side_effects=True),
     )(

time: 65.9 us -> 65.1 us (0.988)
  the two profiles are of different devices: /device:TPU:16 before, /device:TPU:1 now
where the time goes in v4:
time: 65.1 us; the launch traced here: 64.9 us
  Pallas kernels  64.3 us (99%)
    pallas_call x1, Pallas kernels, local(): pl.pallas_call(functools.partial(kernel, sizes), name='delta_rule', out_s...  61.8 us
    pallas_call x1, Pallas kernels, local(): pl.pallas_call(deliver, name='deliver', out_shape=shapes, in_specs=[vmem]...  2.47 us

profile of v4, /device:TPU:1, one launch (start us, length us, event | category | flops | bytes accessed | tf_op | source)
XLA Modules:
  0.0 64.9 jit_solution(18071787668940192847)
XLA Ops:
  0.6 61.8 %delta_rule.1 = (bf16[128,512]{1,0:T(8,128)(2,1)}, bf16[128,512]{1,0:T(8,128)(2,1)}, bf16[128,512]{1,0:T(8,128)(2,1)}, bf16[128,512]{1,0:T(8,128)(2,1)}, f32[4,1...) custom-call(bf16[128,512]{1,0:T(8,128)(2,1)} %bitcast.20, bf16[128,512]{1,0:T(8,128)(2,1)} %bitcast.21, ...), custom_call_target="tpu_custom_call" | custom-call | tf_op jit(solution)/shard_map/delta_rule/pallas_call | solution.py:558
  62.5 2.5 %deliver.1 = (bf16[128,512]{1,0:T(8,128)(2,1)}, bf16[128,512]{1,0:T(8,128)(2,1)}, bf16[128,512]{1,0:T(8,128)(2,1)}, bf16[128,512]{1,0:T(8,128)(2,1)}, f32[4,128]...) custom-call(bf16[128,512]{1,0:T(8,128)(2,1)} %get-tuple-element.21.refs_0_, bf16[128,512]{1,0:T(8,128)(2,1)} %get-tuple-element.22.refs_1_, ...), custom_call_target="tpu_custom_call" | custom-call | tf_op jit(solution)/shard_map/deliver/pallas_call | solution.py:600
